TPU v7x, 512 devices: a whole 4x4x16 slice. The times are simulated.
512 devices in a mesh: chan: 64 (over y_lo, z, core), loc: 8 (over y_hi, x).
Axes of the slice: x: 4, y: 4 (y_hi: 2, y_lo: 2; y = y_hi * 2 + y_lo), z: 16, core: 2. Of those that a mesh axis runs over, the one named last changes fastest.
Arguments:
- pixels: bfloat16 [2048, 256, 256], P('loc', 'chan'), may hold values from -6 to 6
- patch_mask: int32 [2048, 256], P('loc', 'chan'), may hold values 0 or 1
- group_map: int32 [256], replicated, may hold values from 0 to 63, as said below
- embed_weight: bfloat16 [256, 2048], P(None, 'loc'), may hold values from -0.375 to 0.375
- mask_token: bfloat16 [2048], replicated, may hold values from -6 to 6
- chan_embed: bfloat16 [256, 2048], P('chan'), may hold values from -3 to 3
- agg_weight: float32 [256], P('chan'), may hold values from 0.5 to 2
- query_key: bfloat16 [16, 2048], replicated, may hold values from -0.02734375 to 0.02734375
- group_bias: float32 [16, 64], replicated, may hold values from -0.5 to 255
- norm_gain: float32 [2048], replicated, may hold values from 0.25 to 1.75
- head_weight: bfloat16 [2048, 256, 256], P(None, 'chan'), may hold values from -0.125 to 0.125
- head_bias: float32 [256, 256], P('chan'), may hold values from -3 to 3
Outputs:
- rebuilt: bfloat16 [2048, 256, 256], P('loc', 'chan')
Inputs may be any that keep to these rules, and one draw needn't show every extreme that they name: `group_map`: the 4 channels of each bundle (channels k * 4 to k * 4 + 3) name at most two distinct groups.
All inputs are finite; a program needn't handle non-finite values. No bound on the sum of `patch_mask` on one device may be relied on, other than what follows from the above.
Results may differ from a plain program's by a relative error of at most 0.0051.
Values may be sent and summed in bfloat16 or wider, within the bound.
A program may use at most 64 MiB of HBM per device.

v0:
```python
import jax
import jax.numpy as jnp
from jax import lax
from jax.sharding import PartitionSpec as P

C = 256
E = 2048
G = 64
H = 16
BUNDLE = 4


def in_order(blocks, dim):
    blocks = jnp.moveaxis(blocks, 0, dim)
    dims = blocks.shape
    return blocks.reshape(*dims[:dim], dims[dim] * dims[dim + 1], *dims[dim + 2 :])


def copy_for_each(x, axis):
    peers = lax.axis_size(axis)
    return lax.all_to_all(jnp.broadcast_to(x[None], (peers, *x.shape)), axis, 0, 0, tiled=True)


def gathered_copies(x, axis, dim):
    return in_order(copy_for_each(x, axis), dim)


def slot_tables(group_map):
    bundled = group_map.reshape(C // BUNDLE, BUNDLE)
    lowest = jnp.min(bundled, axis=1)
    highest = jnp.max(bundled, axis=1)
    slot_index = (bundled != lowest[:, None]).astype(jnp.int32)
    choose = slot_index[:, None, :] == jnp.arange(2, dtype=jnp.int32)[None, :, None]
    slot_group = jnp.stack([lowest, highest], axis=1).reshape(C // 2)
    to_group = jnp.arange(G, dtype=jnp.int32)[:, None] == slot_group[None, :]
    return (choose.astype(jnp.bfloat16), to_group.astype(jnp.bfloat16))


def attend(aggregate, query_key, group_bias, norm_gain):
    row_count = aggregate.shape[0]
    scores = (
        jnp.einsum(
            "lge,he->lhg", aggregate, query_key.astype(jnp.float32), precision=lax.Precision.HIGHEST
        )
        + group_bias[None]
    )
    weights = jax.nn.softmax(scores, axis=-1)
    pooled = jnp.einsum(
        "lhg,lghd->lhd",
        weights,
        aggregate.reshape(row_count, G, H, E // H),
        precision=lax.Precision.HIGHEST,
    ).reshape(row_count, E)
    inverse_rms = lax.rsqrt(jnp.mean(pooled * pooled, axis=-1, keepdims=True) + 1e-06)
    return (pooled * inverse_rms * norm_gain[None]).astype(jnp.bfloat16)


def shards(
    pixels,
    patch_mask,
    group_map,
    embed_weight,
    mask_token,
    chan_embed,
    agg_weight,
    query_key,
    group_bias,
    norm_gain,
    head_weight,
    head_bias,
):
    loc_count, own_channels, pixel_count = pixels.shape
    peer_count = lax.axis_size("chan")
    per_peer = loc_count // peer_count
    choose, to_group = slot_tables(group_map)
    source_pixels, source_mask = (pixels, patch_mask)
    source_offsets, source_weights = (chan_embed, agg_weight)
    loc_rows, channel_count, _ = source_pixels.shape
    flat_pixels = source_pixels.reshape(loc_rows * channel_count, pixel_count)
    hidden_mask = source_mask.reshape(loc_rows, channel_count, 1) == 1
    section = gathered_copies(embed_weight, "loc", 1)
    columns = section.shape[1]
    projected = jnp.dot(flat_pixels, section, preferred_element_type=jnp.float32).reshape(
        loc_rows, channel_count, columns
    )
    mask_row = mask_token.astype(jnp.float32)
    offset = source_offsets.astype(jnp.float32)
    pre_act = jnp.where(hidden_mask, mask_row[None, None, :], projected) + offset[None]
    weighted = jax.nn.gelu(pre_act, approximate=False) * source_weights[None, :, None]
    weighted = weighted.astype(jnp.bfloat16).reshape(loc_rows * channel_count, columns)
    feature_count = weighted.shape[1]
    local_bundles = channel_count // BUNDLE
    own_choose = lax.dynamic_slice_in_dim(
        choose, lax.axis_index("chan") * local_bundles, local_bundles, 0
    )
    bundled = weighted.reshape(loc_rows, local_bundles, BUNDLE, feature_count)
    bundle_sums = jnp.einsum(
        "lbke,bsk->lbse", bundled, own_choose, preferred_element_type=jnp.float32
    )
    bundle_sums = bundle_sums.astype(jnp.bfloat16).reshape(
        peer_count, per_peer, channel_count // 2, feature_count
    )
    aggregate = jnp.einsum(
        "gq,lqe->lge",
        to_group,
        lax.all_to_all(bundle_sums, "chan", split_axis=0, concat_axis=2, tiled=True)[0],
        preferred_element_type=jnp.float32,
    )
    joined_tokens = attend(aggregate, query_key, group_bias, norm_gain)[None]
    joined_tokens = joined_tokens.reshape(per_peer, feature_count)
    flat_heads = head_weight.reshape(feature_count, own_channels * pixel_count)
    flat_bias = head_bias.reshape(1, own_channels * pixel_count)
    section = gathered_copies(joined_tokens, "chan", 0)
    decoded = jnp.dot(section, flat_heads, preferred_element_type=jnp.float32) + flat_bias
    return decoded.astype(jnp.bfloat16).reshape(section.shape[0], own_channels, pixel_count)


def solution(mesh):
    return jax.shard_map(
        shards,
        mesh=mesh,
        in_specs=(
            P("loc", "chan", None),
            P("loc", "chan"),
            P(),
            P(None, "loc"),
            P(),
            P("chan", None),
            P("chan"),
            P(),
            P(),
            P(),
            P(None, "chan", None),
            P("chan", None),
        ),
        out_specs=P("loc", "chan", None),
        check_vma=False,
    )
```

profile of v0, /device:TPU:1, one launch (start us, length us, event | category | flops | bytes accessed | tf_op | source)
XLA Modules:
  0.0 241.4 jit_solution(7471235654607036802)
XLA Ops:
  0.0 2.0 broadcast_in_dim.24
  2.0 7.5 %all-to-all-start = ((bf16[8,256,256]{2,1,0:T(8,128)(2,1)}), bf16[8,256,256]{2,1,0:T(8,128)(2,1)S(1)}, u32[]{:S(2)}, u32[]{:S(2)}) async-start(bf16[8,256,256]{2,1,0:T(8,128)(2,1)} %broadcast_in_dim.24), calls=%async_computation | async-start | bytes 2097152 | tf_op jit(solution)/shard_map/all_to_all | solution.py:21
  9.5 0.8 reshape.108
  10.3 0.7 convert_element_type.40
  11.0 0.7 convert_element_type.39
  11.7 0.1 fusion.43
  11.9 0.7 broadcast_compare_fusion
  12.6 14.1 %all-to-all-done = bf16[8,256,256]{2,1,0:T(8,128)(2,1)S(1)} async-done(((bf16[8,256,256]{2,1,0:T(8,128)(2,1)}), bf16[8,256,256]{2,1,0:T(8,128)(2,1)S(1)}, u32[]{:S(2)}, u32[]{:S(2)}) %all-to-all-start) | async-done | bytes 1048608 | tf_op jit(solution)/shard_map/all_to_all | solution.py:21
  26.7 0.6 copy.26
  27.3 0.5 reshape.117
  27.9 20.8 %fusion.4 = bf16[256,4,2048]{2,0,1:T(8,128)(2,1)S(1)} fusion(bf16[256,2048,1]{1,0,2:T(8,128)(2,1)S(1)} %reshape.117, f32[4]{0:T(128)S(1)} %copy-done.5, f32[4,2048]{1,0:T(4,128)S(1)} %convert_element_type.40, f32[2048]{0:T(1024)S(1)} %convert_element_type.39, pred[256,4]{0,1:T(4,128)(4,1)S(1)} %broadcast_compare_fusion, bf16[256,4,256]{2,1,0:T(4,128)(2,1)S(1)} %copy-done.4), kind=kOutput, calls=%fused_computation.5 | convolution fusion | flops 1216348160 | bytes 5809168 | tf_op jit(solution)/shard_map/dot_general | solution.py:83
  48.7 4.0 %fusion.14 = bf16[2,256,2048]{2,0,1:T(2,128)(2,1)} fusion(bf16[256,4,2048]{2,0,1:T(8,128)(2,1)S(1)} %fusion.4, s32[1,4]{1,0:T(1,128)S(1)} %constant_dynamic-slice_fusion), kind=kOutput, calls=%fused_computation.24 | convolution fusion | flops 9437192 | bytes 6291472 | tf_op jit(solution)/shard_map/lbke,bsk->lbse/dot_general | solution.py:97
  52.7 16.7 %all-to-all-start.1 = ((bf16[64,4,2,2048]{3,2,1,0:T(2,128)(2,1)}), bf16[64,4,2,2048]{3,2,1,0:T(2,128)(2,1)S(1)}, u32[]{:S(2)}, u32[]{:S(2)}) async-start(bf16[64,4,2,2048]{3,2,1,0:T(2,128)(2,1)} %bitcast.65), calls=%async_computation.1 | async-start | bytes 4194304 | tf_op jit(solution)/shard_map/all_to_all | solution.py:106
  69.4 0.1 copy.30
  69.5 0.1 eq.41
  69.6 94.2 %all-to-all-done.1 = bf16[64,4,2,2048]{3,2,1,0:T(2,128)(2,1)S(1)} async-done(((bf16[64,4,2,2048]{3,2,1,0:T(2,128)(2,1)}), bf16[64,4,2,2048]{3,2,1,0:T(2,128)(2,1)S(1)}, u32[]{:S(2)}, u32[]{:S(2)}) %all-to-all-start.1) | async-done | bytes 2097184 | tf_op jit(solution)/shard_map/all_to_all | solution.py:106
  163.8 3.0 %copy.29 = bf16[1,4,64,2,2048]{4,3,2,1,0:T(2,128)(2,1)} copy(bf16[1,4,64,2,2048]{4,3,1,2,0:T(2,128)(2,1)S(1)} %bitcast.61) | data formatting | bytes 4194304 | tf_op jit(solution)/shard_map/all_to_all | solution.py:106
  166.8 2.8 %squeeze.3 = bf16[4,128,2048]{2,1,0:T(8,128)(2,1)S(1)} reshape(bf16[1,4,64,2,2048]{4,3,2,1,0:T(2,128)(2,1)} %copy.29) | data formatting | bytes 4194304 | tf_op jit(solution)/shard_map/squeeze | solution.py:106
  169.6 0.5 fusion.36
  170.1 1.3 fusion.28
  171.4 0.7 fusion.44
  172.1 0.1 broadcast_divide_fusion
  172.2 1.9 fusion.17
  174.0 0.1 multiply_reduce_fusion
  174.2 0.1 fusion.34
  174.3 1.5 broadcast_in_dim.26
  175.7 10.5 %all-to-all-start.2 = ((bf16[64,4,2048]{2,1,0:T(4,128)(2,1)}), bf16[64,4,2048]{2,1,0:T(4,128)(2,1)S(1)}, u32[]{:S(2)}, u32[]{:S(2)}) async-start(bf16[64,4,2048]{2,1,0:T(4,128)(2,1)} %broadcast_in_dim.26), calls=%async_computation.2 | async-start | bytes 2097152 | tf_op jit(solution)/shard_map/all_to_all | solution.py:21
  186.2 5.2 %copy.36 = bf16[256,8,4,256]{3,1,2,0:T(8,128)(2,1)} copy(bf16[256,8,4,256]{3,2,1,0:T(4,128)(2,1)} %bitcast.62) | data formatting | bytes 8388608
  191.4 45.1 %all-to-all-done.2 = bf16[64,4,2048]{2,1,0:T(4,128)(2,1)S(1)} async-done(((bf16[64,4,2048]{2,1,0:T(4,128)(2,1)}), bf16[64,4,2048]{2,1,0:T(4,128)(2,1)S(1)}, u32[]{:S(2)}, u32[]{:S(2)}) %all-to-all-start.2) | async-done | bytes 1048608 | tf_op jit(solution)/shard_map/all_to_all | solution.py:21
  236.5 0.3 reshape.114
  236.8 3.4 %fusion.22 = bf16[256,1024]{1,0:T(8,128)(2,1)S(1)} fusion(bf16[256,2048]{1,0:T(8,128)(2,1)S(1)} %reshape.114, bf16[2048,1024]{1,0:T(8,128)(2,1)} %bitcast.63, f32[1024]{0:T(1024)S(1)} %bitcast.71), kind=kOutput, calls=%fused_computation.31 | convolution fusion | flops 1074266112 | bytes 5771264 | tf_op jit(solution)/shard_map/dot_general | solution.py:114
  240.2 1.2 reshape.116
  (17 shorter events, 0.1 us)
Async XLA Ops:
  0.0 170.1 %copy-start = (bf16[16,2048]{1,0:T(8,128)(2,1)S(1)}, bf16[16,2048]{1,0:T(8,128)(2,1)}, u32[]{:S(2)}) copy-start(bf16[16,2048]{1,0:T(8,128)(2,1)} %param.19) | copy-start | bytes 196612
  0.0 27.9 %copy-start.4 = (bf16[256,4,256]{2,1,0:T(4,128)(2,1)S(1)}, bf16[256,4,256]{2,1,0:T(4,128)(2,1)}, u32[]{:S(2)}) copy-start(bf16[256,4,256]{2,1,0:T(4,128)(2,1)} %param.12) | copy-start | bytes 1572868
  0.0 27.9 %copy-start.5 = (f32[4]{0:T(128)S(1)}, f32[4]{0:T(128)}, u32[]{:S(2)}) copy-start(f32[4]{0:T(128)} %param.18) | copy-start | bytes 52
  2.0 24.7 %all-to-all-start = ((bf16[8,256,256]{2,1,0:T(8,128)(2,1)}), bf16[8,256,256]{2,1,0:T(8,128)(2,1)S(1)}, u32[]{:S(2)}, u32[]{:S(2)}) async-start(bf16[8,256,256]{2,1,0:T(8,128)(2,1)} %broadcast_in_dim.24), calls=%async_computation | async-start | bytes 2097152 | tf_op jit(solution)/shard_map/all_to_all | solution.py:21
  52.7 111.1 %all-to-all-start.1 = ((bf16[64,4,2,2048]{3,2,1,0:T(2,128)(2,1)}), bf16[64,4,2,2048]{3,2,1,0:T(2,128)(2,1)S(1)}, u32[]{:S(2)}, u32[]{:S(2)}) async-start(bf16[64,4,2,2048]{3,2,1,0:T(2,128)(2,1)} %bitcast.65), calls=%async_computation.1 | async-start | bytes 4194304 | tf_op jit(solution)/shard_map/all_to_all | solution.py:106
  166.8 3.3 %copy-start.1 = (f32[16,64]{1,0:T(8,128)S(1)}, f32[16,64]{1,0:T(8,128)}, u32[]{:S(2)}) copy-start(f32[16,64]{1,0:T(8,128)} %param.20) | copy-start | bytes 12292
  169.5 4.6 %copy-start.2 = (f32[2048]{0:T(1024)S(1)}, f32[2048]{0:T(1024)}, u32[]{:S(2)}) copy-start(f32[2048]{0:T(1024)} %param.21) | copy-start | bytes 24580
  175.7 60.7 %all-to-all-start.2 = ((bf16[64,4,2048]{2,1,0:T(4,128)(2,1)}), bf16[64,4,2048]{2,1,0:T(4,128)(2,1)S(1)}, u32[]{:S(2)}, u32[]{:S(2)}) async-start(bf16[64,4,2048]{2,1,0:T(4,128)(2,1)} %broadcast_in_dim.26), calls=%async_computation.2 | async-start | bytes 2097152 | tf_op jit(solution)/shard_map/all_to_all | solution.py:21
  186.2 5.2 %copy-start.3 = (f32[4,256]{1,0:T(4,128)S(1)}, f32[4,256]{1,0:T(4,128)}, u32[]{:S(2)}) copy-start(f32[4,256]{1,0:T(4,128)} %param.23) | copy-start | bytes 12292
where the time goes:
time: 245 us; the launch traced here: 241 us
  waiting for transfers between devices  153 us (62%)
  starting transfers between devices  34.6 us (14%)
  matrix products  31.9 us (13%)
  local copies, waits for them, and re-layouts  18 us (7%)
  other arithmetic  3.28 us (1%)
    all_to_all x1, waiting for transfers between devices, shards(): lax.all_to_all(bundle_sums, 'chan', split_axis=0, concat_axis=2, tiled=True)  94.2 us
    all_to_all x2, waiting for transfers between devices, copy_for_each(): lax.all_to_all(jnp.broadcast_to(x[None], (peers, *x.shape)), axis, 0, 0,...  59.2 us
    dot_general x1, matrix products, shards(): jnp.dot(flat_pixels, section, preferred_element_type=jnp.float32)  20.8 us
    all_to_all x2, starting transfers between devices, copy_for_each(): lax.all_to_all(jnp.broadcast_to(x[None], (peers, *x.shape)), axis, 0, 0,...  17.9 us
    all_to_all x1, starting transfers between devices, shards(): lax.all_to_all(bundle_sums, 'chan', split_axis=0, concat_axis=2, tiled=True)  16.7 us
    unnamed x14, local copies, waits for them, and re-layouts  5.19 us
  transfers between devices with their start and end apart: 3, of which 3 were waited for; matrix products, arithmetic and copies ran while one was open for 4% of the time, Pallas kernels for 0%

commit v1 on v0

v1 whole, which is shorter than its diff:
```python
import math

import jax
import jax.numpy as jnp
from jax import lax
from jax.sharding import PartitionSpec as P

C = 256
E = 2048
G = 64
H = 16
BUNDLE = 4


def shards(
    pixels,
    patch_mask,
    group_map,
    embed_weight,
    mask_token,
    chan_embed,
    agg_weight,
    query_key,
    group_bias,
    norm_gain,
    head_weight,
    head_bias,
):
    locs, own_channels, pixel_count = pixels.shape
    peers = lax.axis_size("chan")
    bundled = group_map.reshape(C // BUNDLE, BUNDLE)
    lowest = jnp.min(bundled, axis=1)
    highest = jnp.max(bundled, axis=1)
    slot_group = jnp.stack([lowest, highest], axis=1)
    me = lax.axis_index("chan")
    own = lax.dynamic_slice_in_dim(bundled, me, 1, 0)[0]
    own_slot = (own != jnp.min(own)).astype(jnp.int32)
    choose = own_slot[None, :] == jnp.arange(2)[:, None]

    loc_peers = lax.axis_size("loc")
    copies = lax.all_to_all(
        jnp.broadcast_to(embed_weight[None], (loc_peers, *embed_weight.shape)), "loc", 0, 0, tiled=True
    )
    weight = jnp.moveaxis(copies, 0, 1).reshape(pixel_count, E)
    projected = jnp.dot(
        pixels.reshape(locs * own_channels, pixel_count), weight, preferred_element_type=jnp.float32
    ).reshape(locs, own_channels, E)
    hidden = (patch_mask == 1)[:, :, None]
    pre = jnp.where(hidden, mask_token.astype(jnp.float32)[None, None], projected)
    pre = pre + chan_embed.astype(jnp.float32)[None]
    weighted = pre * (1.0 + lax.erf(pre * (1.0 / math.sqrt(2.0)))) * (0.5 * agg_weight)[None, :, None]
    weighted = weighted.astype(jnp.bfloat16)
    sums = jnp.einsum(
        "lke,sk->sle", weighted, choose.astype(jnp.bfloat16), preferred_element_type=jnp.float32
    ).astype(jnp.bfloat16)
    part = jnp.einsum("sle,he->slh", sums, query_key, preferred_element_type=jnp.float32)
    part = part.reshape(2, locs * H)
    every = lax.all_gather(part, "chan", axis=0, tiled=True)
    to_group = (jnp.arange(G)[:, None] == slot_group.reshape(-1)[None]).astype(jnp.float32)
    scores = jnp.dot(to_group, every, precision=lax.Precision.HIGHEST).reshape(G, locs, H)
    scores = scores + group_bias.T[:, None, :]
    attn = jax.nn.softmax(scores, axis=0)
    own_group = jnp.stack([jnp.min(own), jnp.max(own)])
    own_attn = jnp.take(attn, own_group, axis=0)
    pooled = (sums.reshape(2, locs, H, E // H) * own_attn[..., None]).sum(0).reshape(locs, E)
    pooled = lax.psum_scatter(pooled, "chan", scatter_dimension=0, tiled=True)
    inverse = lax.rsqrt(jnp.mean(pooled * pooled, axis=-1, keepdims=True) + 1e-06)
    joined = (pooled * inverse * norm_gain[None]).astype(jnp.bfloat16)
    joined = lax.all_gather(joined, "chan", axis=0, tiled=True)
    decoded = jnp.dot(
        joined, head_weight.reshape(E, own_channels * pixel_count), preferred_element_type=jnp.float32
    )
    decoded = decoded + head_bias.reshape(1, own_channels * pixel_count)
    return decoded.astype(jnp.bfloat16).reshape(locs, own_channels, pixel_count)


def solution(mesh):
    return jax.shard_map(
        shards,
        mesh=mesh,
        in_specs=(
            P("loc", "chan", None),
            P("loc", "chan"),
            P(),
            P(None, "loc"),
            P(),
            P("chan", None),
            P("chan"),
            P(),
            P(),
            P(),
            P(None, "chan", None),
            P("chan", None),
        ),
        out_specs=P("loc", "chan", None),
        check_vma=False,
    )
```

time: 245 us -> 765 us (3.12)
  waiting for transfers between devices: 153 us -> 677 us
  starting transfers between devices: 34.6 us -> 7.81 us
  matrix products: 31.9 us -> 13 us
  other arithmetic: 3.28 us -> 21 us
  between operations: 0.17 us -> 14 us
  local copies, waits for them, and re-layouts: 18 us -> 31.6 us
    unnamed x0 -> x4, waiting for transfers between devices: none -> 436 us
    all_gather x0 -> x2, waiting for transfers between devices: none -> 229 us  [the longest x1 119 us: shards(): every = lax.all_gather(part, 'chan', axis=0, tiled=True)]
    all_to_all x3 -> x1, waiting for transfers between devices: 153 us -> 12.3 us  [shards(): lax.all_to_all(jnp.broadcast_to(embed_weight[None], (loc_peers, *embed_we...]
    all_to_all x3 -> x1, starting transfers between devices: 34.6 us -> 7.47 us  [shards(): lax.all_to_all(jnp.broadcast_to(embed_weight[None], (loc_peers, *embed_we...]
    dot_general x6 -> x5, matrix products: 31.9 us -> 13 us  [the longest x1 3.44 us: shards(): jnp.dot(joined, head_weight.reshape(E, own_channels * pixel_count), prefe...]
    reduce_sum x1 -> x3, other arithmetic: 0.12 us -> 12.4 us  [the longest x1 10 us: shards(): (sums.reshape(2, locs, H, E // H) * own_attn[..., None]).sum(0)]
    mul x0 -> x2, local copies, waits for them, and re-layouts: none -> 8.52 us  [shards(): sums.reshape(2, locs, H, E // H) * own_attn[..., None]]
  transfers between devices with their start and end apart: 3 -> 4, of which waited for: 3 -> 4; matrix products, arithmetic and copies ran while one was open for 4% -> 2% of each run, Pallas kernels for 0% -> 0%
where the time goes in v1:
time: 765 us
  waiting for transfers between devices  677 us (88%)
  local copies, waits for them, and re-layouts  31.6 us (4%)
  other arithmetic  21 us (3%)
  between operations  14 us (2%)
  matrix products  13 us (2%)
  starting transfers between devices  7.81 us (1%)
    unnamed x4, waiting for transfers between devices  436 us
    all_gather x1, waiting for transfers between devices, shards(): every = lax.all_gather(part, 'chan', axis=0, tiled=True)  119 us
    all_gather x1, waiting for transfers between devices, shards(): joined = lax.all_gather(joined, 'chan', axis=0, tiled=True)  110 us
  transfers between devices with their start and end apart: 4, of which 4 were waited for; matrix products, arithmetic and copies ran while one was open for 2% of the time, Pallas kernels for 0%

profile of v1, /device:TPU:1, one launch (start us, length us, event | category | flops | bytes accessed | tf_op | source)
XLA Modules:
  0.0 764.5 jit_solution(2735376849102494480)
XLA Ops:
  6.5 2.0 broadcast_in_dim.27
  8.6 7.5 all-to-all-start
  16.1 0.8 reshape.155
  16.9 0.7 convert_element_type.27
  17.6 0.7 convert_element_type.26
  20.2 0.7 broadcast_compare_fusion
  20.9 12.3 %all-to-all-done = bf16[8,256,256]{2,1,0:T(8,128)(2,1)S(1)} async-done(((bf16[8,256,256]{2,1,0:T(8,128)(2,1)}), bf16[8,256,256]{2,1,0:T(8,128)(2,1)S(1)}, u32[]{:S(2)}, u32[]{:S(2)}) %all-to-all-start) | async-done | bytes 1048608 | tf_op jit(solution)/shard_map/all_to_all | solution.py:41
  34.4 3.0 multiply_convert_fusion
  37.4 3.0 fusion.2
  40.5 1.4 copy-done.1
  41.8 1.2 fusion.5
  43.1 0.8 reshape.170
  45.1 1.3 fusion.17
  46.4 1.3 compare_and_fusion
  47.7 119.1 %all-gather.5.cloned.1.call-done = f32[64,2,4096]{2,1,0:T(2,128)} async-done(((f32[1,2,4096]{2,1,0:T(2,128)}), f32[64,2,4096]{2,1,0:T(2,128)}) %all-gather.5.cloned.1.call-update) | async-done | bytes 2097168 | tf_op jit(solution)/shard_map/all_gather | solution.py:58
  166.8 2.7 reshape.171
  169.5 2.4 fusion.22
  172.0 1.4 exponential_reduce_fusion
  173.6 1.8 copy.46
  175.5 1.4 copy.48
  178.0 2.6 mul.56
  180.6 5.9 mul.57
  186.5 10.0 %multiply_reduce_fusion = f32[256,2048]{1,0:T(8,128)} fusion(f32[2,256,2048]{2,0,1:T(2,128)} %mul.57, bf16[2,256,2048]{2,0,1:T(2,128)(2,1)S(1)} %copy-done.2), kind=kLoop, calls=%fused_computation.2 | loop fusion | flops 2621440 | bytes 8388608 | tf_op jit(solution)/shard_map/reduce_sum | solution.py:65
  196.8 1.3 dynamic-slice
  198.7 435.7 %all-reduce.3.cloned.1.call-done = f32[256,2048]{1,0:T(8,128)} async-done(((f32[256,2048]{1,0:T(8,128)}), f32[256,2048]{1,0:T(8,128)}) %all-reduce.3.cloned.1.call-update) | async-done | bytes 2097168
  634.4 1.0 multiply_reduce_fusion.1
  635.4 1.5 fusion.11
  637.0 5.2 copy.56
  642.2 109.9 %all-gather.7.cloned.1.call-done = bf16[64,4,2048]{2,1,0:T(4,128)(2,1)} async-done(((bf16[1,4,2048]{2,1,0:T(4,128)(2,1)}), bf16[64,4,2048]{2,1,0:T(4,128)(2,1)}) %all-gather.7.cloned.1.call-update) | async-done | bytes 1048592 | tf_op jit(solution)/shard_map/all_gather | solution.py:69
  752.1 1.3 reshape.173
  753.4 3.4 fusion.7
  756.8 1.2 reshape.160
  (42 shorter events, 6.0 us)
Async XLA Ops:
  6.5 35.3 %copy-start = (bf16[16,2048]{1,0:T(8,128)(2,1)S(1)}, bf16[16,2048]{1,0:T(8,128)(2,1)}, u32[]{:S(2)}) copy-start(bf16[16,2048]{1,0:T(8,128)(2,1)} %param.19) | copy-start | bytes 196612
  6.5 27.9 %copy-start.6 = (bf16[256,4,256]{2,1,0:T(4,128)(2,1)S(1)}, bf16[256,4,256]{2,1,0:T(4,128)(2,1)}, u32[]{:S(2)}) copy-start(bf16[256,4,256]{2,1,0:T(4,128)(2,1)} %param.12) | copy-start | bytes 1572868
  8.6 24.7 %all-to-all-start = ((bf16[8,256,256]{2,1,0:T(8,128)(2,1)}), bf16[8,256,256]{2,1,0:T(8,128)(2,1)S(1)}, u32[]{:S(2)}, u32[]{:S(2)}) async-start(bf16[8,256,256]{2,1,0:T(8,128)(2,1)} %broadcast_in_dim.27), calls=%async_computation | async-start | bytes 2097152 | tf_op jit(solution)/shard_map/all_to_all | solution.py:41
  16.0 150.8 %all-gather.5.cloned.1.call-start = ((), (), s32[]{:S(2)}) async-start(), calls=%async_computation.1 | async-start | bytes 2129920 | tf_op jit(solution)/shard_map/all_gather | solution.py:58
  37.4 6.9 copy-start.3
  40.4 1.4 copy-start.1
  43.9 590.6 %all-reduce.3.cloned.1.call-start = ((), (), s32[]{:S(2)}) async-start(), calls=%async_computation.3 | async-start | bytes 4194304
  180.6 5.9 copy-start.2
  186.5 448.9 %copy-start.4 = (f32[2048]{0:T(1024)S(1)}, f32[2048]{0:T(1024)}, u32[]{:S(2)}) copy-start(f32[2048]{0:T(1024)} %param.21) | copy-start | bytes 24580
  196.5 555.5 %all-gather.7.cloned.1.call-start = ((), (), s32[]{:S(2)}) async-start(), calls=%async_computation.2 | async-start | bytes 1064960 | tf_op jit(solution)/shard_map/all_gather | solution.py:69
  637.0 5.2 copy-start.5
Sparse Core Ops, SparseCore 0:
  44.0 122.8 all-gather.4
  196.7 437.7 all-reduce.2
  637.1 114.9 all-gather.6

commit v2 on v1

v2 whole, which is shorter than its diff:
```python
import functools
import math

import jax
import jax.numpy as jnp
from jax import lax
from jax.experimental import pallas as pl
from jax.experimental.pallas import tpu as pltpu
from jax.sharding import PartitionSpec as P

C = 256
E = 2048
G = 64
H = 16
BUNDLE = 4
LOCS = 256
CHAN = 64
ZS = 16
BLOCK = 256
BF = jnp.bfloat16
F32 = jnp.float32
MESH = pl.DeviceIdType.MESH


def split(value, parts):
    pieces = []
    for _ in range(parts - 1):
        piece = value.astype(BF)
        pieces.append(piece)
        value = value - piece.astype(F32)
    return [*pieces, value.astype(BF)]


def exact_dot(onehot, value):
    return sum(jnp.dot(onehot, piece, preferred_element_type=F32) for piece in split(value, 3))


def kernel(
    px,
    aux,
    emb,
    token,
    ce,
    agg,
    gm_s,
    gm_v,
    qk,
    bias,
    gain,
    out,
    wg,
    b,
    pre,
    acc,
    expand,
    sbuf,
    rbuf,
    obuf,
    abuf,
    lhs,
    ps,
    pr,
    own,
    ys,
    yr,
    zs,
    zr,
    zf,
    ssb,
    ssr,
    jt,
    esem,
    rsem,
    psem,
    ssem,
    srsem,
    csem,
    crsem,
    yrsem,
    zrsem,
    qrsem,
    jsem,
    jz,
    jy,
    jc,
    jd,
):
    ci = lax.axis_index("chan")
    li = lax.axis_index("loc")
    core = ci % 2
    z = (ci // 2) % ZS
    ylo = ci // (2 * ZS)
    x = li % 4
    yhi = li // 4
    way = 1 - 2 * core
    partner = ci + way
    ypartner = (ci + 2 * ZS) % CHAN
    nxt = yhi * 4 + (x + way + 4) % 4
    prv = yhi * 4 + (x - way + 4) % 4
    cross_loc = (1 - yhi) * 4 + x

    def at(chan, loc=None):
        return {"chan": chan, "loc": li if loc is None else loc}

    def rdma(src, dst, send, recv, where):
        return pltpu.make_async_remote_copy(
            src_ref=src, dst_ref=dst, send_sem=send, recv_sem=recv, device_id=where, device_id_type=MESH
        )

    def await_bytes(ref, sem):
        pltpu.make_async_copy(ref, ref, sem).wait()

    barrier = pltpu.get_barrier_semaphore()
    pl.semaphore_signal(barrier, inc=1, device_id=at(ci, nxt), device_id_type=MESH)
    pl.semaphore_signal(barrier, inc=1, device_id=at(ci, prv), device_id_type=MESH)
    pl.semaphore_signal(barrier, inc=1, device_id=at(ypartner, cross_loc), device_id_type=MESH)

    @pl.loop(1, CHAN)
    def _(d):
        pl.semaphore_signal(barrier, inc=1, device_id=at((ci + d) % CHAN), device_id_type=MESH)

    def place(t, row):
        return ((yhi + row) % 2) * 4 + (x + way * ((3 * t * t - 5 * t) // 2) + 8) % 4

    swapped = {1: 1, 2: 4, 3: 5, 4: 2, 5: 3, 6: 6, 7: 7}

    def half(step):
        return wg.at[place(step // 2, step % 2), core]

    def pass_on(step, to, loc):
        rdma(half(step), half(step), esem.at[0], rsem.at[to], at(ci, loc)).start()

    def to_partner(step):
        rdma(half(step), half(step), esem.at[0], psem.at[swapped[step]], at(partner)).start()

    def arrived(step):
        await_bytes(half(step), rsem.at[step])

    base = ci * BUNDLE
    groups = [gm_s[base + k] for k in range(BUNDLE)]
    low = jnp.minimum(jnp.minimum(groups[0], groups[1]), jnp.minimum(groups[2], groups[3]))
    weights = []
    for k in range(BUNDLE):
        full = 0.5 * agg[k]
        second = jnp.where(groups[k] != low, full, 0.0)
        weights.append((full - second, second))

    wg[li] = emb[...].reshape(2, 128, BLOCK)
    acc[...] = jnp.zeros_like(acc)
    zr[z] = jnp.zeros((8, 1024), BF)
    row16 = lax.broadcasted_iota(jnp.int32, (128, BLOCK), 0)

    @pl.loop(0, 8)
    def _(step):
        @pl.when(step == 1)
        def _():
            pl.semaphore_wait(barrier, CHAN - 1 + 3)
            mine = emb.at[pl.ds(pl.multiple_of(core * 128, 128), 128), :]
            dst = wg.at[li, core]
            rdma(mine, dst, esem.at[0], rsem.at[1], at(ypartner, cross_loc)).start()
            rdma(mine, dst, esem.at[0], rsem.at[2], at(ci, nxt)).start()
            rdma(mine, dst, esem.at[0], rsem.at[4], at(ci, prv)).start()
            arrived(1)
            pass_on(1, 3, nxt)
            pass_on(1, 5, prv)
            to_partner(1)
            arrived(2)
            pass_on(2, 6, nxt)
            to_partner(2)
            arrived(4)
            to_partner(4)

        @pl.when(step == 3)
        def _():
            arrived(3)
            pass_on(3, 7, nxt)
            to_partner(3)
            arrived(5)
            to_partner(5)

        @pl.when(step == 5)
        def _():
            arrived(6)
            to_partner(6)

        @pl.when(step == 6)
        def _():
            arrived(7)
            to_partner(7)

        t, row = step // 2, step % 2
        j = place(t, row)

        @pl.when(step > 0)
        def _():
            await_bytes(wg.at[j, 1 - core], psem.at[step])

        columns = pl.ds(pl.multiple_of(j * BLOCK, BLOCK), BLOCK)
        weight = wg[j].reshape(BLOCK, BLOCK)
        extra = jnp.where(row16 == 0, token[:, columns].astype(F32), 0.0)
        embeds = ce[:, columns].astype(F32)
        for k in range(BUNDLE):
            extra = jnp.where(row16 == 1 + k, embeds[k : k + 1], extra)
        extra = extra.astype(BF)

        @pl.loop(0, BUNDLE)
        def _(k):
            rows = pl.ds(pl.multiple_of(k * LOCS, LOCS), LOCS)
            pre[rows, :] = jnp.dot(px[rows, :], weight, preferred_element_type=F32) + jnp.dot(
                aux[rows, :], extra, preferred_element_type=F32
            )

        @pl.loop(0, LOCS // 32)
        def _(chunk):
            first, second = None, None
            for k in range(BUNDLE):
                v = pre[pl.ds(pl.multiple_of(k * LOCS + chunk * 32, 32), 32), :]
                g = v + v * lax.erf(v * (1.0 / math.sqrt(2.0)))
                w0, w1 = weights[k]
                first = g * w0 if first is None else first + g * w0
                second = g * w1 if second is None else second + g * w1
            b[j, pl.ds(pl.multiple_of(chunk * 32, 32), 32), :] = first.astype(BF)
            b[j, pl.ds(pl.multiple_of(LOCS + chunk * 32, 32), 32), :] = second.astype(BF)

        q = jnp.concatenate([qk[:, columns]] * 8, axis=0)
        acc[...] += lax.dot_general(b[j], q, (((1,), (1,)), ((), ())), preferred_element_type=F32)
        p = lax.broadcasted_iota(jnp.int32, (BLOCK, BLOCK), 0) % H
        head = 2 * step + lax.broadcasted_iota(jnp.int32, (BLOCK, BLOCK), 1) // 128
        expand[step] = jnp.where(p == head, 1.0, 0.0).astype(BF)

    lane = lax.broadcasted_iota(jnp.int32, (CHAN, 128), 1)
    part = jnp.zeros((CHAN, 128), F32)
    for q in range(8):
        part = part + jnp.where(lane // H == q, acc[q * 64 : (q + 1) * 64, :], 0.0)
    sbuf[...] = part.reshape(CHAN, 1, 128)

    @pl.loop(1, CHAN)
    def _(d):
        peer = (ci + d) % CHAN
        rdma(sbuf.at[peer], rbuf.at[ci], ssem.at[0], srsem.at[0], at(peer)).start()

    rbuf[ci] = sbuf[ci]
    gmap = jnp.broadcast_to(gm_v[...].astype(F32), (8, C))
    wide = lax.broadcasted_iota(jnp.int32, (CHAN, C), 1)
    bund = lax.broadcasted_iota(jnp.int32, (CHAN, C), 0)
    inside = wide // BUNDLE == bund
    lows = jnp.min(jnp.where(inside, gmap[0:1], 1e9), axis=1, keepdims=True)
    highs = jnp.max(jnp.where(inside, gmap[0:1], -1.0), axis=1, keepdims=True)
    gcol = lax.broadcasted_iota(jnp.int32, (CHAN, G), 1).astype(F32)
    from_group = [jnp.where(v == gcol, 1.0, 0.0).astype(BF) for v in (lows, highs)]
    to_group = [f.astype(F32).T.astype(BF) for f in from_group]

    await_bytes(rbuf.at[pl.ds(0, CHAN - 1)], srsem.at[0])
    got = rbuf[...].reshape(CHAN, 128)
    mixed = jnp.where(lane < 64, exact_dot(to_group[0], got), exact_dot(to_group[1], got))
    scores = mixed + pltpu.roll(mixed, 64, 1) + bias[...]
    top = jnp.max(scores, axis=0, keepdims=True)
    raised = jnp.exp(scores - top)
    attn = raised / jnp.sum(raised, axis=0, keepdims=True)
    back = jnp.where(lane < 64, exact_dot(from_group[0], attn), exact_dot(from_group[1], attn))
    obuf[...] = back.reshape(CHAN, 1, 128)

    @pl.loop(1, CHAN)
    def _(d):
        peer = (ci + d) % CHAN
        rdma(obuf.at[peer], abuf.at[ci], ssem.at[1], srsem.at[1], at(peer)).start()

    abuf[ci] = obuf[ci]
    await_bytes(abuf.at[pl.ds(0, CHAN - 1)], srsem.at[1])
    high, rest = split(abuf[...].reshape(CHAN, 128), 2)
    high, rest = high.astype(F32), rest.astype(F32)
    for q in range(8):
        lhs[q * 64 : (q + 1) * 64, 0:128] = jnp.where(lane // H == q, high, 0.0).astype(BF)
        lhs[q * 64 : (q + 1) * 64, 128:256] = jnp.where(lane // H == q, rest, 0.0).astype(BF)

    def weigh(j):
        spread = jnp.dot(lhs[...], expand[j], preferred_element_type=F32)
        return spread[:LOCS] * b[j, 0:LOCS, :].astype(F32) + spread[LOCS:] * b[j, LOCS:, :].astype(F32)

    @pl.loop(0, 4)
    def _(t):
        ps[t] = weigh((1 - core) * 4 + t).astype(BF)
        rdma(ps.at[t], pr.at[t], csem.at[0], crsem.at[t], at(partner)).start()

    @pl.loop(0, 4)
    def _(t):
        own[t] = weigh(core * 4 + t)

    @pl.loop(0, 4)
    def _(t):
        await_bytes(pr.at[t], crsem.at[t])
        theirs = pl.ds(pl.multiple_of((1 - ylo) * 128, 128), 128)
        ys[t] = (own[t, theirs, :] + pr[t, theirs, :].astype(F32)).astype(BF)
        rdma(ys.at[t], yr.at[t], csem.at[1], yrsem.at[t], at(ypartner)).start()

    for t in range(4):
        mine = pl.ds(pl.multiple_of(ylo * 128, 128), 128)
        await_bytes(yr.at[t], yrsem.at[t])
        total = own[t, mine, :] + pr[t, mine, :].astype(F32) + yr[t].astype(F32)
        total = total.reshape(ZS, 8, BLOCK)
        zf[:, :, t * BLOCK : (t + 1) * BLOCK] = total
        zs[:, :, t * BLOCK : (t + 1) * BLOCK] = total.astype(BF)

    @pl.loop(1, ZS)
    def _(e):
        d = (e % 2) * ((e + 1) // 2) + (1 - e % 2) * (ZS - e // 2)
        to = (z + d) % ZS
        peer = ylo * 2 * ZS + to * 2 + core
        rdma(zs.at[to], zr.at[z], csem.at[2], zrsem.at[0], at(peer)).start()

    await_bytes(zr.at[pl.ds(0, ZS - 1)], zrsem.at[0])
    pooled = zf[z]
    for k in range(ZS):
        pooled = pooled + zr[k].astype(F32)
    squares = jnp.sum(pooled * pooled, axis=1, keepdims=True)
    ssb[...] = jnp.broadcast_to(squares, (8, 128))
    share = rdma(ssb, ssr, csem.at[3], qrsem.at[0], at(partner))
    share.start()
    scaled = pooled * gain[:, pl.ds(pl.multiple_of(core * 1024, 1024), 1024)]
    share.wait_recv()
    inverse = lax.rsqrt((squares + ssr[:, 0:1]) * (1.0 / E) + 1e-06)
    jt[core, ylo, z] = (scaled * inverse).astype(BF)

    @pl.loop(1, ZS)
    def _(e):
        d = (e % 2) * ((e + 1) // 2) + (1 - e % 2) * (ZS - e // 2)
        peer = ylo * 2 * ZS + ((z + d) % ZS) * 2 + core
        block = jt.at[core, ylo, z]
        rdma(block, block, jsem.at[0], jz.at[d], at(peer)).start()

    @pl.loop(0, ZS)
    def _(e):
        d = ((e % 2) * ((e + 1) // 2) + (1 - e % 2) * (ZS - e // 2)) % ZS
        block = jt.at[core, ylo, (z + ZS - d) % ZS]

        @pl.when(e > 0)
        def _():
            await_bytes(block, jz.at[d])

        rdma(block, block, jsem.at[1], jy.at[d], at(ypartner)).start()
        rdma(block, block, jsem.at[2], jc.at[d], at(partner)).start()

    @pl.loop(0, ZS)
    def _(e):
        d = ((e % 2) * ((e + 1) // 2) + (1 - e % 2) * (ZS - e // 2)) % ZS
        block = jt.at[core, 1 - ylo, (z + ZS - d) % ZS]
        await_bytes(block, jy.at[d])
        rdma(block, block, jsem.at[2], jd.at[d], at(partner)).start()

    @pl.loop(0, ZS)
    def _(d):
        block = (z + ZS - d) % ZS
        await_bytes(jt.at[1 - core, ylo, block], jc.at[d])
        await_bytes(jt.at[1 - core, 1 - ylo, block], jd.at[d])

    for c in range(2):
        out[:, c * 1024 : (c + 1) * 1024] = jt[c].reshape(LOCS, 1024)

    await_bytes(wg.at[pl.ds(0, 7)], esem.at[0])
    await_bytes(sbuf.at[pl.ds(0, CHAN - 1)], ssem.at[0])
    await_bytes(obuf.at[pl.ds(0, CHAN - 1)], ssem.at[1])
    await_bytes(ps, csem.at[0])
    await_bytes(ys, csem.at[1])
    await_bytes(zs.at[pl.ds(0, ZS - 1)], csem.at[2])
    share.wait_send()
    await_bytes(jt.at[0, 0, pl.ds(0, ZS - 1)], jsem.at[0])
    await_bytes(jt.at[0, 0], jsem.at[1])
    await_bytes(jt.at[0], jsem.at[2])


def shards(
    pixels,
    patch_mask,
    group_map,
    embed_weight,
    mask_token,
    chan_embed,
    agg_weight,
    query_key,
    group_bias,
    norm_gain,
    head_weight,
    head_bias,
):
    locs, own_channels, pixel_count = pixels.shape
    hidden = (patch_mask == 1).T[:, :, None]
    px = jnp.where(hidden, jnp.zeros((), BF), jnp.swapaxes(pixels, 0, 1))
    at_lane = lax.broadcasted_iota(jnp.int32, (own_channels, locs, 128), 2)
    channel = lax.broadcasted_iota(jnp.int32, (own_channels, locs, 128), 0)
    aux = ((at_lane == channel + 1) | ((at_lane == 0) & hidden)).astype(BF)
    bias = jnp.tile(group_bias.T, (1, 8))
    vmem = pl.BlockSpec(memory_space=pltpu.VMEM)
    smem = pl.BlockSpec(memory_space=pltpu.SMEM)
    dma = pltpu.SemaphoreType.DMA
    joined = pl.pallas_call(
        kernel,
        out_shape=jax.ShapeDtypeStruct((LOCS, E), BF),
        in_specs=[vmem] * 5 + [smem] * 2 + [vmem] * 4,
        out_specs=vmem,
        scratch_shapes=[
            pltpu.VMEM((8, 2, 128, BLOCK), BF),
            pltpu.VMEM((8, 2 * LOCS, BLOCK), BF),
            pltpu.VMEM((BUNDLE * LOCS, BLOCK), F32),
            pltpu.VMEM((2 * LOCS, 128), F32),
            pltpu.VMEM((8, BLOCK, BLOCK), BF),
            pltpu.VMEM((CHAN, 1, 128), F32),
            pltpu.VMEM((CHAN, 1, 128), F32),
            pltpu.VMEM((CHAN, 1, 128), F32),
            pltpu.VMEM((CHAN, 1, 128), F32),
            pltpu.VMEM((2 * LOCS, 256), BF),
            pltpu.VMEM((4, LOCS, BLOCK), BF),
            pltpu.VMEM((4, LOCS, BLOCK), BF),
            pltpu.VMEM((4, LOCS, BLOCK), F32),
            pltpu.VMEM((4, 128, BLOCK), BF),
            pltpu.VMEM((4, 128, BLOCK), BF),
            pltpu.VMEM((ZS, 8, 1024), BF),
            pltpu.VMEM((ZS, 8, 1024), BF),
            pltpu.VMEM((ZS, 8, 1024), F32),
            pltpu.VMEM((8, 128), F32),
            pltpu.VMEM((8, 128), F32),
            pltpu.VMEM((2, 2, ZS, 8, 1024), BF),
            dma((1,)),
            dma((8,)),
            dma((8,)),
            dma((2,)),
            dma((2,)),
            dma((4,)),
            dma((4,)),
            dma((4,)),
            dma((1,)),
            dma((1,)),
            dma((3,)),
            dma((ZS,)),
            dma((ZS,)),
            dma((ZS,)),
            dma((ZS,)),
        ],
        compiler_params=pltpu.CompilerParams(
            collective_id=0, has_side_effects=True, vmem_limit_bytes=32 * 1024 * 1024
        ),
    )(
        px.reshape(own_channels * locs, pixel_count),
        aux.reshape(own_channels * locs, 128),
        embed_weight,
        mask_token.reshape(1, E),
        chan_embed,
        agg_weight,
        group_map,
        group_map.reshape(1, C),
        query_key,
        bias,
        norm_gain.reshape(1, E),
    )
    decoded = jnp.dot(
        joined, head_weight.reshape(E, own_channels * pixel_count), preferred_element_type=F32
    )
    decoded = decoded + head_bias.reshape(1, own_channels * pixel_count)
    return decoded.astype(BF).reshape(locs, own_channels, pixel_count)


def solution(mesh):
    return jax.shard_map(
        shards,
        mesh=mesh,
        in_specs=(
            P("loc", "chan", None),
            P("loc", "chan"),
            P(),
            P(None, "loc"),
            P(),
            P("chan", None),
            P("chan"),
            P(),
            P(),
            P(),
            P(None, "chan", None),
            P("chan", None),
        ),
        out_specs=P("loc", "chan", None),
        check_vma=False,
    )
```

time: 765 us -> 114 us (0.15)
  the two profiles are of different devices: /device:TPU:1 before, /device:TPU:41 now
where the time goes in v2:
time: 114 us
  Pallas kernels  98.7 us (87%)
  local copies, waits for them, and re-layouts  11.4 us (10%)
  other arithmetic  2.51 us (2%)
  matrix products  1.28 us (1%)
    pallas_call x1, Pallas kernels, shards(): pl.pallas_call(kernel, out_shape=jax.ShapeDtypeStruct((LOCS, E), BF), in_...  98.7 us
    unnamed x16, local copies, waits for them, and re-layouts  8.47 us

profile of v2, /device:TPU:41, one launch (start us, length us, event | category | flops | bytes accessed | tf_op | source)
XLA Modules:
  0.0 113.9 jit_solution(18088432727446230550)
XLA Ops:
  0.0 0.7 compare_bitcast_fusion
  0.7 0.1 broadcast_bitcast_fusion
  0.8 0.7 copy.21
  1.5 0.7 reshape.29.token
  2.2 0.2 copy.16
  2.4 0.7 tile.4
  3.1 0.1 copy.18.bias
  3.1 0.4 fusion.2.aux
  3.5 1.4 %bitcast_select_fusion = bf16[4,256,256]{2,0,1:T(4,128)(2,1)S(1)} fusion(bf16[256,4,256]{2,1,0:T(4,128)(2,1)} %param.12, pred[4,256]{0,1:T(8,128)(4,1)S(1)} %copy.16), kind=kLoop, calls=%fused_computation.2 | loop fusion | flops 262144 | bytes 1049600 | tf_op jit(solution)/shard_map/jit(_where)/select_n | solution.py:387
  4.9 0.1 copy.17
  5.0 0.0 copy-start
  5.0 0.9 copy-done
  5.9 0.0 copy-start.1
  5.9 0.8 copy-done.1
  6.8 0.0 copy-start.2
  6.8 0.7 copy-done.2
  7.5 0.0 copy-start.3
  7.5 0.7 copy-done.3
  8.2 0.0 copy-start.4
  8.2 0.7 copy-done.4
  8.9 0.0 copy-start.5
  8.9 0.7 copy-done.5
  9.5 98.7 %shard_map.118 = bf16[256,2048]{1,0:T(8,128)(2,1)S(1)} custom-call(bf16[1024,256]{1,0:T(8,128)(2,1)S(1)} %bitcast.18, bf16[1024,128]{1,0:T(8,128)(2,1)S(1)} %fusion.2.aux, bf16[256,256]{1,0:T(8,128)(2,1)S(1)} %copy-done, bf16[1,2048]{1,0:T(2,128)(2,1)S(1)} %reshape.29.token, bf16[4,2048]{1,0:T(4,128)(2,1)S(1)} %copy-done.2, f32[4]{0:T(128)S(1)} %copy-done.5, ...), custom_call_target="tpu_custom_call" | custom-call | tf_op jit(solution)/shard_map/pallas_call | solution.py:395
  108.3 3.2 %copy.20 = bf16[256,8,4,256]{3,1,2,0:T(8,128)(2,1)S(1)} copy(bf16[256,8,4,256]{3,2,1,0:T(4,128)(2,1)} %bitcast.21) | data formatting | bytes 8388608
  111.5 1.3 %fusion = bf16[256,1024]{1,0:T(8,128)(2,1)S(1)} fusion(bf16[256,2048]{1,0:T(8,128)(2,1)S(1)} %shard_map.118, bf16[2048,1024]{1,0:T(8,128)(2,1)S(1)} %bitcast.22, f32[1024]{0:T(1024)S(1)} %bitcast.27), kind=kOutput, calls=%fused_computation.1 | convolution fusion | flops 1074266112 | bytes 5771264 | tf_op jit(solution)/shard_map/dot_general | solution.py:454
  112.8 1.2 %reshape.33 = bf16[256,4,256]{2,1,0:T(4,128)(2,1)} reshape(bf16[256,1024]{1,0:T(8,128)(2,1)S(1)} %fusion) | data formatting | bytes 1048576 | tf_op jit(solution)/shard_map/reshape | solution.py:458
  (4 shorter events, 0.0 us)
Async XLA Ops:
  5.0 0.9 copy-start
  5.9 0.8 copy-start.1
  6.8 0.7 copy-start.2
  7.5 0.7 copy-start.3
  8.2 0.7 copy-start.4
  8.9 0.7 copy-start.5

commit v3 on v2

--- a/solution.py
+++ b/solution.py
@@ -36,18 +36,38 @@
 
 
 def kernel(
-    px,
-    aux,
-    emb,
+    pixels_h,
+    mask_h,
+    emb_h,
+    token_h,
+    ce_h,
+    agg_h,
+    map_h,
+    gmv_h,
+    qk_h,
+    gbias_h,
+    gain_h,
+    head_h,
+    hbias_h,
+    out,
+    raw,
+    maskv,
     token,
     ce,
     agg,
     gm_s,
     gm_v,
     qk,
-    bias,
+    gbias,
     gain,
-    out,
+    hraw,
+    hbias,
+    tokf,
+    keep,
+    px,
+    aux,
+    wd,
+    dec,
     wg,
     b,
     pre,
@@ -64,11 +84,15 @@
     ys,
     yr,
     zs,
+    zf,
     zr,
-    zf,
+    rin,
+    rout,
+    pooled,
     ssb,
     ssr,
     jt,
+    lsem,
     esem,
     rsem,
     psem,
@@ -77,6 +101,8 @@
     csem,
     crsem,
     yrsem,
+    zsem,
+    rinsem,
     zrsem,
     qrsem,
     jsem,
@@ -119,6 +145,28 @@
     def _(d):
         pl.semaphore_signal(barrier, inc=1, device_id=at((ci + d) % CHAN), device_id_type=MESH)
 
+    def load(k, src, dst):
+        copy = pltpu.make_async_copy(src, dst, lsem.at[k])
+        copy.start()
+        return copy
+
+    first_half = load(0, emb_h.at[pl.ds(0, 128)], wg.at[li, 0])
+    other_half = load(1, emb_h.at[pl.ds(128, 128)], wg.at[li, 1])
+    loads = [
+        load(2, pixels_h, raw),
+        load(3, mask_h, maskv),
+        load(4, token_h, token),
+        load(5, ce_h, ce),
+        load(6, agg_h, agg),
+        load(7, map_h, gm_s),
+        load(8, gmv_h, gm_v),
+        load(9, qk_h, qk),
+        load(10, gbias_h, gbias),
+        load(11, gain_h, gain),
+        load(12, hbias_h, hbias),
+    ]
+    heads = load(13, head_h, hraw)
+
     def place(t, row):
         return ((yhi + row) % 2) * 4 + (x + way * ((3 * t * t - 5 * t) // 2) + 8) % 4
 
@@ -135,6 +183,11 @@
 
     def arrived(step):
         await_bytes(half(step), rsem.at[step])
+
+    for copy in loads:
+        copy.wait()
+    first_half.wait()
+    other_half.wait()
 
     base = ci * BUNDLE
     groups = [gm_s[base + k] for k in range(BUNDLE)]
@@ -145,9 +198,32 @@
         second = jnp.where(groups[k] != low, full, 0.0)
         weights.append((full - second, second))
 
-    wg[li] = emb[...].reshape(2, 128, BLOCK)
     acc[...] = jnp.zeros_like(acc)
-    zr[z] = jnp.zeros((8, 1024), BF)
+    tokf[...] = token[...].astype(F32)
+
+    @pl.loop(0, BUNDLE)
+    def _(c):
+        hid = jnp.broadcast_to(maskv[pl.ds(c, 1), :].astype(F32), (128, LOCS)).T
+        rows = pl.ds(pl.multiple_of(c * LOCS, LOCS), LOCS)
+        at_lane = lax.broadcasted_iota(jnp.int32, (LOCS, 128), 1)
+        aux[rows, :] = jnp.where(at_lane == 0, hid, jnp.where(at_lane == 1 + c, 1.0, 0.0)).astype(BF)
+        keep[c] = 1.0 - hid
+
+    @pl.loop(0, LOCS // 32)
+    def _(i):
+        rows = pl.ds(pl.multiple_of(i * 32, 32), 32)
+        turned = jnp.swapaxes(raw[rows], 0, 1)
+        for c in range(BUNDLE):
+            shown = keep[c, rows, :]
+            kept = turned[c].astype(F32) * jnp.concatenate([shown, shown], axis=1)
+            px[pl.ds(pl.multiple_of(c * LOCS + i * 32, 32), 32), :] = kept.astype(BF)
+
+    @pl.loop(0, 8)
+    def _(step):
+        p = lax.broadcasted_iota(jnp.int32, (BLOCK, BLOCK), 0) % H
+        head = 2 * step + lax.broadcasted_iota(jnp.int32, (BLOCK, BLOCK), 1) // 128
+        expand[step] = jnp.where(p == head, 1.0, 0.0).astype(BF)
+
     row16 = lax.broadcasted_iota(jnp.int32, (128, BLOCK), 0)
 
     @pl.loop(0, 8)
@@ -155,8 +231,8 @@
         @pl.when(step == 1)
         def _():
             pl.semaphore_wait(barrier, CHAN - 1 + 3)
-            mine = emb.at[pl.ds(pl.multiple_of(core * 128, 128), 128), :]
-            dst = wg.at[li, core]
+            mine = wg.at[li, core]
+            dst = mine
             rdma(mine, dst, esem.at[0], rsem.at[1], at(ypartner, cross_loc)).start()
             rdma(mine, dst, esem.at[0], rsem.at[2], at(ci, nxt)).start()
             rdma(mine, dst, esem.at[0], rsem.at[4], at(ci, prv)).start()
@@ -197,7 +273,8 @@
 
         columns = pl.ds(pl.multiple_of(j * BLOCK, BLOCK), BLOCK)
         weight = wg[j].reshape(BLOCK, BLOCK)
-        extra = jnp.where(row16 == 0, token[:, columns].astype(F32), 0.0)
+        hide = jnp.concatenate([tokf[pl.ds(2 * j, 1), :], tokf[pl.ds(2 * j + 1, 1), :]], axis=1)
+        extra = jnp.where(row16 == 0, hide, 0.0)
         embeds = ce[:, columns].astype(F32)
         for k in range(BUNDLE):
             extra = jnp.where(row16 == 1 + k, embeds[k : k + 1], extra)
@@ -224,9 +301,6 @@
 
         q = jnp.concatenate([qk[:, columns]] * 8, axis=0)
         acc[...] += lax.dot_general(b[j], q, (((1,), (1,)), ((), ())), preferred_element_type=F32)
-        p = lax.broadcasted_iota(jnp.int32, (BLOCK, BLOCK), 0) % H
-        head = 2 * step + lax.broadcasted_iota(jnp.int32, (BLOCK, BLOCK), 1) // 128
-        expand[step] = jnp.where(p == head, 1.0, 0.0).astype(BF)
 
     lane = lax.broadcasted_iota(jnp.int32, (CHAN, 128), 1)
     part = jnp.zeros((CHAN, 128), F32)
@@ -250,10 +324,18 @@
     from_group = [jnp.where(v == gcol, 1.0, 0.0).astype(BF) for v in (lows, highs)]
     to_group = [f.astype(F32).T.astype(BF) for f in from_group]
 
+    bias = jnp.concatenate([gbias[...]] * 8, axis=0).T
+    heads.wait()
+
+    @pl.loop(0, E // 32)
+    def _(i):
+        rows = pl.ds(pl.multiple_of(i * 32, 32), 32)
+        wd[:, rows, :] = jnp.swapaxes(hraw[rows], 0, 1)
+
     await_bytes(rbuf.at[pl.ds(0, CHAN - 1)], srsem.at[0])
     got = rbuf[...].reshape(CHAN, 128)
     mixed = jnp.where(lane < 64, exact_dot(to_group[0], got), exact_dot(to_group[1], got))
-    scores = mixed + pltpu.roll(mixed, 64, 1) + bias[...]
+    scores = mixed + pltpu.roll(mixed, 64, 1) + bias
     top = jnp.max(scores, axis=0, keepdims=True)
     raised = jnp.exp(scores - top)
     attn = raised / jnp.sum(raised, axis=0, keepdims=True)
@@ -293,75 +375,115 @@
         ys[t] = (own[t, theirs, :] + pr[t, theirs, :].astype(F32)).astype(BF)
         rdma(ys.at[t], yr.at[t], csem.at[1], yrsem.at[t], at(ypartner)).start()
 
-    for t in range(4):
+    def zdev(to):
+        return at(ylo * 2 * ZS + to * 2 + core)
+
+    @pl.loop(0, 4)
+    def _(t):
         mine = pl.ds(pl.multiple_of(ylo * 128, 128), 128)
         await_bytes(yr.at[t], yrsem.at[t])
         total = own[t, mine, :] + pr[t, mine, :].astype(F32) + yr[t].astype(F32)
         total = total.reshape(ZS, 8, BLOCK)
-        zf[:, :, t * BLOCK : (t + 1) * BLOCK] = total
-        zs[:, :, t * BLOCK : (t + 1) * BLOCK] = total.astype(BF)
-
-    @pl.loop(1, ZS)
-    def _(e):
-        d = (e % 2) * ((e + 1) // 2) + (1 - e % 2) * (ZS - e // 2)
-        to = (z + d) % ZS
-        peer = ylo * 2 * ZS + to * 2 + core
-        rdma(zs.at[to], zr.at[z], csem.at[2], zrsem.at[0], at(peer)).start()
-
-    await_bytes(zr.at[pl.ds(0, ZS - 1)], zrsem.at[0])
-    pooled = zf[z]
-    for k in range(ZS):
-        pooled = pooled + zr[k].astype(F32)
-    squares = jnp.sum(pooled * pooled, axis=1, keepdims=True)
+        zf[t] = total
+        zs[t] = total.astype(BF)
+        for d in (8, 7, 6, 5):
+            to, via = (z + d) % ZS, (z + d - 4) % ZS
+            rdma(zs.at[t, to], rin.at[t, 0, d - 5], zsem.at[0], rinsem.at[0, t], zdev(via)).start()
+            if d < 8:
+                to, via = (z + ZS - d) % ZS, (z + ZS - d + 4) % ZS
+                rdma(zs.at[t, to], rin.at[t, 1, d - 5], zsem.at[0], rinsem.at[1, t], zdev(via)).start()
+        for d in (3, 2, 1):
+            for q, to in enumerate(((z + d) % ZS, (z + ZS - d) % ZS)):
+                rdma(zs.at[t, to], zr.at[t, q, d - 1], zsem.at[0], zrsem.at[t], zdev(to)).start()
+
+    @pl.loop(0, 4)
+    def _(t):
+        for q, to, n in ((0, (z + 4) % ZS, 4), (1, (z + ZS - 4) % ZS, 3)):
+            await_bytes(rin.at[t, q, pl.ds(0, n)], rinsem.at[q, t])
+            total = zf[t, to]
+            for d in range(n):
+                total = total + rin[t, q, d].astype(F32)
+            rout[t, q] = total.astype(BF)
+            rdma(rout.at[t, q], zr.at[t, q, 3], zsem.at[1], zrsem.at[t], zdev(to)).start()
+
+    squares = jnp.zeros((8, 1), F32)
+    for t in range(4):
+        await_bytes(zr.at[t], zrsem.at[t])
+        total = zf[t, z]
+        for q in range(2):
+            for d in range(4):
+                total = total + zr[t, q, d].astype(F32)
+        pooled[:, t * BLOCK : (t + 1) * BLOCK] = total
+        squares = squares + jnp.sum(total * total, axis=1, keepdims=True)
     ssb[...] = jnp.broadcast_to(squares, (8, 128))
     share = rdma(ssb, ssr, csem.at[3], qrsem.at[0], at(partner))
     share.start()
-    scaled = pooled * gain[:, pl.ds(pl.multiple_of(core * 1024, 1024), 1024)]
+    scaled = pooled[...] * gain[:, pl.ds(pl.multiple_of(core * 1024, 1024), 1024)]
     share.wait_recv()
     inverse = lax.rsqrt((squares + ssr[:, 0:1]) * (1.0 / E) + 1e-06)
     jt[core, ylo, z] = (scaled * inverse).astype(BF)
 
-    @pl.loop(1, ZS)
-    def _(e):
-        d = (e % 2) * ((e + 1) // 2) + (1 - e % 2) * (ZS - e // 2)
-        peer = ylo * 2 * ZS + ((z + d) % ZS) * 2 + core
-        block = jt.at[core, ylo, z]
-        rdma(block, block, jsem.at[0], jz.at[d], at(peer)).start()
-
-    @pl.loop(0, ZS)
-    def _(e):
-        d = ((e % 2) * ((e + 1) // 2) + (1 - e % 2) * (ZS - e // 2)) % ZS
-        block = jt.at[core, ylo, (z + ZS - d) % ZS]
-
-        @pl.when(e > 0)
-        def _():
-            await_bytes(block, jz.at[d])
-
+    def row_block(row, d):
+        return jt.at[core, row, (z + ZS - d) % ZS]
+
+    def spread(d, way_z, steps):
+        for n in steps:
+            block = row_block(ylo, d)
+            there = (d + way_z * n) % ZS
+            rdma(block, block, jsem.at[0], jz.at[there], zdev((z + ZS + way_z * n) % ZS)).start()
+
+    def share_block(d):
+        block = row_block(ylo, d)
         rdma(block, block, jsem.at[1], jy.at[d], at(ypartner)).start()
         rdma(block, block, jsem.at[2], jc.at[d], at(partner)).start()
 
-    @pl.loop(0, ZS)
-    def _(e):
-        d = ((e % 2) * ((e + 1) // 2) + (1 - e % 2) * (ZS - e // 2)) % ZS
-        block = jt.at[core, 1 - ylo, (z + ZS - d) % ZS]
+    for n in (4, 3, 2, 1):
+        spread(0, 1, (n,))
+        spread(0, -1, (n,))
+    share_block(0)
+    order = (4, 12, 1, 15, 2, 14, 3, 13, 5, 11, 6, 10, 7, 9, 8)
+    for d in order:
+        await_bytes(row_block(ylo, d), jz.at[d])
+        if d == 4:
+            spread(4, 1, (4, 3, 2, 1))
+        if d == 12:
+            spread(12, -1, (3, 2, 1))
+        share_block(d)
+    for d in (0, *order):
+        block = row_block(1 - ylo, d)
         await_bytes(block, jy.at[d])
         rdma(block, block, jsem.at[2], jd.at[d], at(partner)).start()
 
-    @pl.loop(0, ZS)
-    def _(d):
-        block = (z + ZS - d) % ZS
-        await_bytes(jt.at[1 - core, ylo, block], jc.at[d])
-        await_bytes(jt.at[1 - core, 1 - ylo, block], jd.at[d])
-
-    for c in range(2):
-        out[:, c * 1024 : (c + 1) * 1024] = jt[c].reshape(LOCS, 1024)
+    def decode(row):
+        sides = [jt[c, row].reshape(128, 1024) for c in range(2)]
+
+        @pl.loop(0, BUNDLE)
+        def _(c):
+            total = jnp.dot(sides[0], wd[c, 0:1024, :], preferred_element_type=F32)
+            total = total + jnp.dot(sides[1], wd[c, 1024:2048, :], preferred_element_type=F32)
+            dec[c] = (total + hbias[pl.ds(c, 1), :]).astype(BF)
+
+        @pl.loop(0, 4)
+        def _(i):
+            rows = pl.ds(pl.multiple_of(row * 128 + i * 32, 32), 32)
+            out[rows] = jnp.swapaxes(dec[:, pl.ds(pl.multiple_of(i * 32, 32), 32), :], 0, 1)
+
+    for d in range(ZS):
+        block = jt.at[1 - core, ylo, (z + ZS - d) % ZS]
+        await_bytes(block, jc.at[d])
+    decode(ylo)
+    for d in range(ZS):
+        block = jt.at[1 - core, 1 - ylo, (z + ZS - d) % ZS]
+        await_bytes(block, jd.at[d])
+    decode(1 - ylo)
 
     await_bytes(wg.at[pl.ds(0, 7)], esem.at[0])
     await_bytes(sbuf.at[pl.ds(0, CHAN - 1)], ssem.at[0])
     await_bytes(obuf.at[pl.ds(0, CHAN - 1)], ssem.at[1])
     await_bytes(ps, csem.at[0])
     await_bytes(ys, csem.at[1])
-    await_bytes(zs.at[pl.ds(0, ZS - 1)], csem.at[2])
+    await_bytes(zs.at[:, pl.ds(0, 13)], zsem.at[0])
+    await_bytes(rout, zsem.at[1])
     share.wait_send()
     await_bytes(jt.at[0, 0, pl.ds(0, ZS - 1)], jsem.at[0])
     await_bytes(jt.at[0, 0], jsem.at[1])
@@ -382,22 +504,33 @@
     head_weight,
     head_bias,
 ):
-    locs, own_channels, pixel_count = pixels.shape
-    hidden = (patch_mask == 1).T[:, :, None]
-    px = jnp.where(hidden, jnp.zeros((), BF), jnp.swapaxes(pixels, 0, 1))
-    at_lane = lax.broadcasted_iota(jnp.int32, (own_channels, locs, 128), 2)
-    channel = lax.broadcasted_iota(jnp.int32, (own_channels, locs, 128), 0)
-    aux = ((at_lane == channel + 1) | ((at_lane == 0) & hidden)).astype(BF)
-    bias = jnp.tile(group_bias.T, (1, 8))
     vmem = pl.BlockSpec(memory_space=pltpu.VMEM)
-    smem = pl.BlockSpec(memory_space=pltpu.SMEM)
+    hbm = pl.BlockSpec(memory_space=pltpu.HBM)
     dma = pltpu.SemaphoreType.DMA
-    joined = pl.pallas_call(
+    return pl.pallas_call(
         kernel,
-        out_shape=jax.ShapeDtypeStruct((LOCS, E), BF),
-        in_specs=[vmem] * 5 + [smem] * 2 + [vmem] * 4,
+        out_shape=jax.ShapeDtypeStruct(pixels.shape, BF),
+        in_specs=[hbm] * 13,
         out_specs=vmem,
         scratch_shapes=[
+            pltpu.VMEM((LOCS, BUNDLE, BLOCK), BF),
+            pltpu.VMEM((BUNDLE, LOCS), jnp.int32),
+            pltpu.VMEM((16, 128), BF),
+            pltpu.VMEM((BUNDLE, E), BF),
+            pltpu.SMEM((BUNDLE,), F32),
+            pltpu.SMEM((C,), jnp.int32),
+            pltpu.VMEM((1, C), jnp.int32),
+            pltpu.VMEM((H, E), BF),
+            pltpu.VMEM((H, G), F32),
+            pltpu.VMEM((1, E), F32),
+            pltpu.VMEM((E, BUNDLE, BLOCK), BF),
+            pltpu.VMEM((BUNDLE, BLOCK), F32),
+            pltpu.VMEM((16, 128), F32),
+            pltpu.VMEM((BUNDLE, LOCS, 128), F32),
+            pltpu.VMEM((BUNDLE * LOCS, BLOCK), BF),
+            pltpu.VMEM((BUNDLE * LOCS, 128), BF),
+            pltpu.VMEM((BUNDLE, E, BLOCK), BF),
+            pltpu.VMEM((BUNDLE, 128, BLOCK), BF),
             pltpu.VMEM((8, 2, 128, BLOCK), BF),
             pltpu.VMEM((8, 2 * LOCS, BLOCK), BF),
             pltpu.VMEM((BUNDLE * LOCS, BLOCK), F32),
@@ -413,12 +546,16 @@
             pltpu.VMEM((4, LOCS, BLOCK), F32),
             pltpu.VMEM((4, 128, BLOCK), BF),
             pltpu.VMEM((4, 128, BLOCK), BF),
-            pltpu.VMEM((ZS, 8, 1024), BF),
-            pltpu.VMEM((ZS, 8, 1024), BF),
-            pltpu.VMEM((ZS, 8, 1024), F32),
+            pltpu.VMEM((4, ZS, 8, BLOCK), BF),
+            pltpu.VMEM((4, ZS, 8, BLOCK), F32),
+            pltpu.VMEM((4, 2, 4, 8, BLOCK), BF),
+            pltpu.VMEM((4, 2, 4, 8, BLOCK), BF),
+            pltpu.VMEM((4, 2, 8, BLOCK), BF),
+            pltpu.VMEM((8, 1024), F32),
             pltpu.VMEM((8, 128), F32),
             pltpu.VMEM((8, 128), F32),
             pltpu.VMEM((2, 2, ZS, 8, 1024), BF),
+            dma((14,)),
             dma((1,)),
             dma((8,)),
             dma((8,)),
@@ -427,7 +564,9 @@
             dma((4,)),
             dma((4,)),
             dma((4,)),
-            dma((1,)),
+            dma((2,)),
+            dma((2, 4)),
+            dma((4,)),
             dma((1,)),
             dma((3,)),
             dma((ZS,)),
@@ -436,26 +575,23 @@
             dma((ZS,)),
         ],
         compiler_params=pltpu.CompilerParams(
-            collective_id=0, has_side_effects=True, vmem_limit_bytes=32 * 1024 * 1024
+            collective_id=0, has_side_effects=True, vmem_limit_bytes=56 * 1024 * 1024
         ),
     )(
-        px.reshape(own_channels * locs, pixel_count),
-        aux.reshape(own_channels * locs, 128),
+        pixels,
+        patch_mask.T,
         embed_weight,
-        mask_token.reshape(1, E),
+        mask_token.reshape(16, 128),
         chan_embed,
         agg_weight,
         group_map,
         group_map.reshape(1, C),
         query_key,
-        bias,
+        group_bias,
         norm_gain.reshape(1, E),
+        head_weight,
+        head_bias,
     )
-    decoded = jnp.dot(
-        joined, head_weight.reshape(E, own_channels * pixel_count), preferred_element_type=F32
-    )
-    decoded = decoded + head_bias.reshape(1, own_channels * pixel_count)
-    return decoded.astype(BF).reshape(locs, own_channels, pixel_count)
 
 
 def solution(mesh):

time: 114 us -> 93.1 us (0.82)
  the two profiles are of different devices: /device:TPU:41 before, /device:TPU:1 now
where the time goes in v3:
time: 93.1 us; the launch traced here: 93 us
  Pallas kernels  90.9 us (98%)
  local copies, waits for them, and re-layouts  2.02 us (2%)
    pallas_call x1, Pallas kernels, shards(): pl.pallas_call(kernel, out_shape=jax.ShapeDtypeStruct(pixels.shape, BF),...  90.9 us
    unnamed x1, local copies, waits for them, and re-layouts  2.02 us

profile of v3, /device:TPU:1, one launch (start us, length us, event | category | flops | bytes accessed | tf_op | source)
XLA Modules:
  0.0 93.0 jit_solution(15734089564266718519)
XLA Ops:
  0.0 90.9 %shard_map.118 = bf16[256,4,256]{2,1,0:T(4,128)(2,1)} custom-call(bf16[256,4,256]{2,1,0:T(4,128)(2,1)} %pixels_h.1, s32[4,256]{1,0:T(4,128)} %bitcast.5, bf16[256,256]{1,0:T(8,128)(2,1)} %emb_h.1, bf16[16,128]{1,0:T(8,128)(2,1)} %bitcast.6, bf16[4,2048]{1,0:T(4,128)(2,1)} %ce_h.1, f32[4]{0:T(128)} %agg_h.1, s32[256]{0:T(256)} %map_h.1, s32[1,256]{1,0:T(1,128)} %bitcast.7, ...), custom_call_target="tpu_custom_call" | custom-call | tf_op jit(solution)/shard_map/pallas_call | solution.py:510
  90.9 2.0 %copy.14 = bf16[256,4,256]{2,1,0:T(4,128)(2,1)} copy(bf16[256,4,256]{2,1,0:T(4,128)(2,1)} %shard_map.118) | data formatting | bytes 1048576

commit v4 on v3

--- a/solution.py
+++ b/solution.py
@@ -65,9 +65,7 @@
     tokf,
     keep,
     px,
-    aux,
     wd,
-    dec,
     wg,
     b,
     pre,
@@ -136,14 +134,7 @@
     def await_bytes(ref, sem):
         pltpu.make_async_copy(ref, ref, sem).wait()
 
-    barrier = pltpu.get_barrier_semaphore()
-    pl.semaphore_signal(barrier, inc=1, device_id=at(ci, nxt), device_id_type=MESH)
-    pl.semaphore_signal(barrier, inc=1, device_id=at(ci, prv), device_id_type=MESH)
-    pl.semaphore_signal(barrier, inc=1, device_id=at(ypartner, cross_loc), device_id_type=MESH)
-
-    @pl.loop(1, CHAN)
-    def _(d):
-        pl.semaphore_signal(barrier, inc=1, device_id=at((ci + d) % CHAN), device_id_type=MESH)
+    diagonals = [(1 - yhi) * 4 + n % 4 for n in (nxt, prv)]
 
     def load(k, src, dst):
         copy = pltpu.make_async_copy(src, dst, lsem.at[k])
@@ -152,6 +143,24 @@
 
     first_half = load(0, emb_h.at[pl.ds(0, 128)], wg.at[li, 0])
     other_half = load(1, emb_h.at[pl.ds(128, 128)], wg.at[li, 1])
+
+    def for_peers(act):
+        @pl.loop(0, ZS - 1)
+        def _(e):
+            off = 8 - (e % 2) * ((e + 1) // 2) + (1 - e % 2) * (e // 2)
+            there = ((z + off) % ZS) * 2
+            for side in (1 - ylo, ylo):
+                for c in range(2):
+                    act(side * 2 * ZS + there + c)
+
+        act((1 - ylo) * 2 * ZS + z * 2)
+        act((1 - ylo) * 2 * ZS + z * 2 + 1)
+        act(partner)
+
+    barrier = pltpu.get_barrier_semaphore()
+    for chan, loc in ((ci, nxt), (ci, prv), (ypartner, cross_loc), *((ypartner, d) for d in diagonals)):
+        pl.semaphore_signal(barrier, inc=1, device_id=at(chan, loc), device_id_type=MESH)
+    for_peers(lambda p: pl.semaphore_signal(barrier, inc=1, device_id=at(p), device_id_type=MESH))
     loads = [
         load(2, pixels_h, raw),
         load(3, mask_h, maskv),
@@ -184,10 +193,10 @@
     def arrived(step):
         await_bytes(half(step), rsem.at[step])
 
+    first_half.wait()
+    other_half.wait()
     for copy in loads:
         copy.wait()
-    first_half.wait()
-    other_half.wait()
 
     base = ci * BUNDLE
     groups = [gm_s[base + k] for k in range(BUNDLE)]
@@ -206,7 +215,7 @@
         hid = jnp.broadcast_to(maskv[pl.ds(c, 1), :].astype(F32), (128, LOCS)).T
         rows = pl.ds(pl.multiple_of(c * LOCS, LOCS), LOCS)
         at_lane = lax.broadcasted_iota(jnp.int32, (LOCS, 128), 1)
-        aux[rows, :] = jnp.where(at_lane == 0, hid, jnp.where(at_lane == 1 + c, 1.0, 0.0)).astype(BF)
+        px[rows, BLOCK:] = jnp.where(at_lane == 0, hid, jnp.where(at_lane == 1 + c, 1.0, 0.0)).astype(BF)
         keep[c] = 1.0 - hid
 
     @pl.loop(0, LOCS // 32)
@@ -216,7 +225,7 @@
         for c in range(BUNDLE):
             shown = keep[c, rows, :]
             kept = turned[c].astype(F32) * jnp.concatenate([shown, shown], axis=1)
-            px[pl.ds(pl.multiple_of(c * LOCS + i * 32, 32), 32), :] = kept.astype(BF)
+            px[pl.ds(pl.multiple_of(c * LOCS + i * 32, 32), 32), 0:BLOCK] = kept.astype(BF)
 
     @pl.loop(0, 8)
     def _(step):
@@ -226,66 +235,15 @@
 
     row16 = lax.broadcasted_iota(jnp.int32, (128, BLOCK), 0)
 
-    @pl.loop(0, 8)
-    def _(step):
-        @pl.when(step == 1)
-        def _():
-            pl.semaphore_wait(barrier, CHAN - 1 + 3)
-            mine = wg.at[li, core]
-            dst = mine
-            rdma(mine, dst, esem.at[0], rsem.at[1], at(ypartner, cross_loc)).start()
-            rdma(mine, dst, esem.at[0], rsem.at[2], at(ci, nxt)).start()
-            rdma(mine, dst, esem.at[0], rsem.at[4], at(ci, prv)).start()
-            arrived(1)
-            pass_on(1, 3, nxt)
-            pass_on(1, 5, prv)
-            to_partner(1)
-            arrived(2)
-            pass_on(2, 6, nxt)
-            to_partner(2)
-            arrived(4)
-            to_partner(4)
-
-        @pl.when(step == 3)
-        def _():
-            arrived(3)
-            pass_on(3, 7, nxt)
-            to_partner(3)
-            arrived(5)
-            to_partner(5)
-
-        @pl.when(step == 5)
-        def _():
-            arrived(6)
-            to_partner(6)
-
-        @pl.when(step == 6)
-        def _():
-            arrived(7)
-            to_partner(7)
-
-        t, row = step // 2, step % 2
-        j = place(t, row)
-
-        @pl.when(step > 0)
-        def _():
-            await_bytes(wg.at[j, 1 - core], psem.at[step])
-
+    def embed_block(j):
         columns = pl.ds(pl.multiple_of(j * BLOCK, BLOCK), BLOCK)
-        weight = wg[j].reshape(BLOCK, BLOCK)
         hide = jnp.concatenate([tokf[pl.ds(2 * j, 1), :], tokf[pl.ds(2 * j + 1, 1), :]], axis=1)
         extra = jnp.where(row16 == 0, hide, 0.0)
         embeds = ce[:, columns].astype(F32)
         for k in range(BUNDLE):
             extra = jnp.where(row16 == 1 + k, embeds[k : k + 1], extra)
-        extra = extra.astype(BF)
-
-        @pl.loop(0, BUNDLE)
-        def _(k):
-            rows = pl.ds(pl.multiple_of(k * LOCS, LOCS), LOCS)
-            pre[rows, :] = jnp.dot(px[rows, :], weight, preferred_element_type=F32) + jnp.dot(
-                aux[rows, :], extra, preferred_element_type=F32
-            )
+        weight = jnp.concatenate([wg[j].reshape(BLOCK, BLOCK), extra.astype(BF)], axis=0)
+        pre[...] = jnp.dot(px[...], weight, preferred_element_type=F32)
 
         @pl.loop(0, LOCS // 32)
         def _(chunk):
@@ -302,16 +260,58 @@
         q = jnp.concatenate([qk[:, columns]] * 8, axis=0)
         acc[...] += lax.dot_general(b[j], q, (((1,), (1,)), ((), ())), preferred_element_type=F32)
 
+    embed_block(li)
+    pl.semaphore_wait(barrier, CHAN - 1 + 5)
+    mine = wg.at[li, core]
+    rdma(mine, mine, esem.at[0], rsem.at[2], at(ci, nxt)).start()
+    rdma(mine, mine, esem.at[0], rsem.at[4], at(ci, prv)).start()
+    rdma(mine, mine, esem.at[0], rsem.at[1], at(ypartner, cross_loc)).start()
+    rdma(mine, mine, esem.at[0], rsem.at[3], at(ypartner, diagonals[0])).start()
+    rdma(mine, mine, esem.at[0], rsem.at[5], at(ypartner, diagonals[1])).start()
+
+    @pl.loop(1, 8)
+    def _(step):
+        @pl.when(step == 1)
+        def _():
+            arrived(2)
+            pass_on(2, 6, nxt)
+            to_partner(2)
+            arrived(4)
+            to_partner(4)
+
+        @pl.when(step == 3)
+        def _():
+            arrived(1)
+            to_partner(1)
+            arrived(3)
+            pass_on(3, 7, nxt)
+            to_partner(3)
+            arrived(6)
+            to_partner(6)
+
+        @pl.when(step == 4)
+        def _():
+            arrived(5)
+            to_partner(5)
+
+        @pl.when(step == 6)
+        def _():
+            arrived(7)
+            to_partner(7)
+
+        t, row = step % 4, step // 4
+        j = place(t, row)
+        await_bytes(wg.at[j, 1 - core], psem.at[2 * t + row])
+        embed_block(j)
+
     lane = lax.broadcasted_iota(jnp.int32, (CHAN, 128), 1)
     part = jnp.zeros((CHAN, 128), F32)
     for q in range(8):
         part = part + jnp.where(lane // H == q, acc[q * 64 : (q + 1) * 64, :], 0.0)
-    sbuf[...] = part.reshape(CHAN, 1, 128)
-
-    @pl.loop(1, CHAN)
-    def _(d):
-        peer = (ci + d) % CHAN
-        rdma(sbuf.at[peer], rbuf.at[ci], ssem.at[0], srsem.at[0], at(peer)).start()
+    sbuf[:, 0, :] = part
+    sbuf[:, 1, :] = jnp.concatenate([part[16:32], part[0:16], part[48:64], part[32:48]], axis=0)
+
+    for_peers(lambda p: rdma(sbuf.at[p], rbuf.at[ci], ssem.at[0], srsem.at[0], at(p)).start())
 
     rbuf[ci] = sbuf[ci]
     gmap = jnp.broadcast_to(gm_v[...].astype(F32), (8, C))
@@ -333,23 +333,35 @@
         wd[:, rows, :] = jnp.swapaxes(hraw[rows], 0, 1)
 
     await_bytes(rbuf.at[pl.ds(0, CHAN - 1)], srsem.at[0])
-    got = rbuf[...].reshape(CHAN, 128)
-    mixed = jnp.where(lane < 64, exact_dot(to_group[0], got), exact_dot(to_group[1], got))
-    scores = mixed + pltpu.roll(mixed, 64, 1) + bias
+    lane2 = lax.broadcasted_iota(jnp.int32, (CHAN, 256), 1) % 128
+    got = jnp.concatenate([rbuf[:, 0, :], rbuf[:, 1, :]], axis=1)
+    mixed = jnp.where(lane2 < 64, exact_dot(to_group[0], got), exact_dot(to_group[1], got))
+    turned = [pltpu.roll(mixed[:, k * 128 : (k + 1) * 128], 64, 1) for k in range(2)]
+    scores = mixed + jnp.concatenate(turned, axis=1) + jnp.concatenate([bias, bias], axis=1)
     top = jnp.max(scores, axis=0, keepdims=True)
     raised = jnp.exp(scores - top)
     attn = raised / jnp.sum(raised, axis=0, keepdims=True)
-    back = jnp.where(lane < 64, exact_dot(from_group[0], attn), exact_dot(from_group[1], attn))
-    obuf[...] = back.reshape(CHAN, 1, 128)
-
-    @pl.loop(1, CHAN)
-    def _(d):
-        peer = (ci + d) % CHAN
-        rdma(obuf.at[peer], abuf.at[ci], ssem.at[1], srsem.at[1], at(peer)).start()
-
-    abuf[ci] = obuf[ci]
-    await_bytes(abuf.at[pl.ds(0, CHAN - 1)], srsem.at[1])
-    high, rest = split(abuf[...].reshape(CHAN, 128), 2)
+    back = jnp.where(lane2 < 64, exact_dot(from_group[0], attn), exact_dot(from_group[1], attn))
+    upper = z >= ZS // 2
+    obuf[:, 0, :] = jnp.where(upper, back[:, 128:], back[:, :128])
+    obuf[:, 1, :] = jnp.where(upper, back[:, :128], back[:, 128:])
+    pair = ylo * ZS + (z % (ZS // 2)) * 2 + core
+
+    for off in (12, 3, 13, 2, 14, 1, 15):
+        there = ((z + off) % ZS) * 2
+        for side in (1 - ylo, ylo):
+            for c in range(2):
+                peer = side * 2 * ZS + there + c
+                rdma(obuf.at[peer], abuf.at[pair], ssem.at[1], srsem.at[1], at(peer)).start()
+
+    for peer in ((1 - ylo) * 2 * ZS + z * 2, (1 - ylo) * 2 * ZS + z * 2 + 1, partner):
+        rdma(obuf.at[peer], abuf.at[pair], ssem.at[1], srsem.at[1], at(peer)).start()
+
+    abuf[pair] = obuf[ci]
+    await_bytes(abuf.at[pl.ds(0, 31)], srsem.at[1])
+    low_sets, high_sets = abuf[:, 0, :], abuf[:, 1, :]
+    received = jnp.concatenate([low_sets[0:16], high_sets[0:16], low_sets[16:32], high_sets[16:32]], axis=0)
+    high, rest = split(received, 2)
     high, rest = high.astype(F32), rest.astype(F32)
     for q in range(8):
         lhs[q * 64 : (q + 1) * 64, 0:128] = jnp.where(lane // H == q, high, 0.0).astype(BF)
@@ -366,13 +378,11 @@
 
     @pl.loop(0, 4)
     def _(t):
-        own[t] = weigh(core * 4 + t)
-
-    @pl.loop(0, 4)
-    def _(t):
+        mixed_in = weigh(core * 4 + t)
         await_bytes(pr.at[t], crsem.at[t])
+        own[t] = mixed_in + pr[t].astype(F32)
         theirs = pl.ds(pl.multiple_of((1 - ylo) * 128, 128), 128)
-        ys[t] = (own[t, theirs, :] + pr[t, theirs, :].astype(F32)).astype(BF)
+        ys[t] = own[t, theirs, :].astype(BF)
         rdma(ys.at[t], yr.at[t], csem.at[1], yrsem.at[t], at(ypartner)).start()
 
     def zdev(to):
@@ -382,7 +392,7 @@
     def _(t):
         mine = pl.ds(pl.multiple_of(ylo * 128, 128), 128)
         await_bytes(yr.at[t], yrsem.at[t])
-        total = own[t, mine, :] + pr[t, mine, :].astype(F32) + yr[t].astype(F32)
+        total = own[t, mine, :] + yr[t].astype(F32)
         total = total.reshape(ZS, 8, BLOCK)
         zf[t] = total
         zs[t] = total.astype(BF)
@@ -449,29 +459,26 @@
         if d == 12:
             spread(12, -1, (3, 2, 1))
         share_block(d)
+    def decode(row):
+        sides = [jt[c, row].reshape(128, 1024) for c in range(2)]
+
+        @pl.loop(0, BUNDLE)
+        def _(c):
+            total = jnp.dot(sides[0], wd[c, 0:1024, :], preferred_element_type=F32)
+            total = total + jnp.dot(sides[1], wd[c, 1024:2048, :], preferred_element_type=F32)
+            rows = pl.ds(pl.multiple_of(row * 128, 128), 128)
+            columns = pl.ds(pl.multiple_of(c * BLOCK, BLOCK), BLOCK)
+            out[rows, columns] = (total + hbias[pl.ds(c, 1), :]).astype(BF)
+
+    for d in range(ZS):
+        block = jt.at[1 - core, ylo, (z + ZS - d) % ZS]
+        await_bytes(block, jc.at[d])
+    decode(ylo)
     for d in (0, *order):
         block = row_block(1 - ylo, d)
         await_bytes(block, jy.at[d])
         rdma(block, block, jsem.at[2], jd.at[d], at(partner)).start()
 
-    def decode(row):
-        sides = [jt[c, row].reshape(128, 1024) for c in range(2)]
-
-        @pl.loop(0, BUNDLE)
-        def _(c):
-            total = jnp.dot(sides[0], wd[c, 0:1024, :], preferred_element_type=F32)
-            total = total + jnp.dot(sides[1], wd[c, 1024:2048, :], preferred_element_type=F32)
-            dec[c] = (total + hbias[pl.ds(c, 1), :]).astype(BF)
-
-        @pl.loop(0, 4)
-        def _(i):
-            rows = pl.ds(pl.multiple_of(row * 128 + i * 32, 32), 32)
-            out[rows] = jnp.swapaxes(dec[:, pl.ds(pl.multiple_of(i * 32, 32), 32), :], 0, 1)
-
-    for d in range(ZS):
-        block = jt.at[1 - core, ylo, (z + ZS - d) % ZS]
-        await_bytes(block, jc.at[d])
-    decode(ylo)
     for d in range(ZS):
         block = jt.at[1 - core, 1 - ylo, (z + ZS - d) % ZS]
         await_bytes(block, jd.at[d])
@@ -479,7 +486,7 @@
 
     await_bytes(wg.at[pl.ds(0, 7)], esem.at[0])
     await_bytes(sbuf.at[pl.ds(0, CHAN - 1)], ssem.at[0])
-    await_bytes(obuf.at[pl.ds(0, CHAN - 1)], ssem.at[1])
+    await_bytes(obuf.at[pl.ds(0, 31)], ssem.at[1])
     await_bytes(ps, csem.at[0])
     await_bytes(ys, csem.at[1])
     await_bytes(zs.at[:, pl.ds(0, 13)], zsem.at[0])
@@ -507,9 +514,9 @@
     vmem = pl.BlockSpec(memory_space=pltpu.VMEM)
     hbm = pl.BlockSpec(memory_space=pltpu.HBM)
     dma = pltpu.SemaphoreType.DMA
-    return pl.pallas_call(
+    decoded = pl.pallas_call(
         kernel,
-        out_shape=jax.ShapeDtypeStruct(pixels.shape, BF),
+        out_shape=jax.ShapeDtypeStruct((LOCS, BUNDLE * BLOCK), BF),
         in_specs=[hbm] * 13,
         out_specs=vmem,
         scratch_shapes=[
@@ -527,19 +534,17 @@
             pltpu.VMEM((BUNDLE, BLOCK), F32),
             pltpu.VMEM((16, 128), F32),
             pltpu.VMEM((BUNDLE, LOCS, 128), F32),
-            pltpu.VMEM((BUNDLE * LOCS, BLOCK), BF),
-            pltpu.VMEM((BUNDLE * LOCS, 128), BF),
+            pltpu.VMEM((BUNDLE * LOCS, BLOCK + 128), BF),
             pltpu.VMEM((BUNDLE, E, BLOCK), BF),
-            pltpu.VMEM((BUNDLE, 128, BLOCK), BF),
             pltpu.VMEM((8, 2, 128, BLOCK), BF),
             pltpu.VMEM((8, 2 * LOCS, BLOCK), BF),
             pltpu.VMEM((BUNDLE * LOCS, BLOCK), F32),
             pltpu.VMEM((2 * LOCS, 128), F32),
             pltpu.VMEM((8, BLOCK, BLOCK), BF),
-            pltpu.VMEM((CHAN, 1, 128), F32),
-            pltpu.VMEM((CHAN, 1, 128), F32),
-            pltpu.VMEM((CHAN, 1, 128), F32),
-            pltpu.VMEM((CHAN, 1, 128), F32),
+            pltpu.VMEM((CHAN, 2, 128), F32),
+            pltpu.VMEM((CHAN, 2, 128), F32),
+            pltpu.VMEM((CHAN, 2, 128), F32),
+            pltpu.VMEM((CHAN // 2, 2, 128), F32),
             pltpu.VMEM((2 * LOCS, 256), BF),
             pltpu.VMEM((4, LOCS, BLOCK), BF),
             pltpu.VMEM((4, LOCS, BLOCK), BF),
@@ -575,9 +580,9 @@
             dma((ZS,)),
         ],
         compiler_params=pltpu.CompilerParams(
-            collective_id=0, has_side_effects=True, vmem_limit_bytes=56 * 1024 * 1024
+            collective_id=0, has_side_effects=True, vmem_limit_bytes=32 * 1024 * 1024
         ),
-    )(
+    )(*[pltpu.with_memory_space_constraint(v, pltpu.HBM) for v in (
         pixels,
         patch_mask.T,
         embed_weight,
@@ -591,7 +596,8 @@
         norm_gain.reshape(1, E),
         head_weight,
         head_bias,
-    )
+    )])
+    return decoded.reshape(pixels.shape)
 
 
 def solution(mesh):

time: 93.1 us -> 84.8 us (0.911)
  Pallas kernels: 90.9 us -> 83.5 us
    pallas_call x1, Pallas kernels: 90.9 us -> 83.5 us  [shards(): pl.pallas_call(kernel, out_shape=jax.ShapeDtypeStruct((LOCS, BUNDLE * BLO...]
    unnamed x1 -> x0, local copies, waits for them, and re-layouts: 2.02 us -> none
    reshape x0 -> x1, local copies, waits for them, and re-layouts: none -> 1.17 us  [shards(): return decoded.reshape(pixels.shape)]
where the time goes in v4:
time: 84.8 us; the launch traced here: 84.6 us
  Pallas kernels  83.5 us (98%)
  local copies, waits for them, and re-layouts  1.17 us (1%)
    pallas_call x1, Pallas kernels, shards(): pl.pallas_call(kernel, out_shape=jax.ShapeDtypeStruct((LOCS, BUNDLE * BLO...  83.5 us

profile of v4, /device:TPU:1, one launch (start us, length us, event | category | flops | bytes accessed | tf_op | source)
XLA Modules:
  0.0 84.6 jit_solution(13376925815672187704)
XLA Ops:
  0.0 83.5 %shard_map.118 = bf16[256,1024]{1,0:T(8,128)(2,1)S(1)} custom-call(bf16[256,4,256]{2,1,0:T(4,128)(2,1)} %pixels_h.1, s32[4,256]{1,0:T(4,128)} %bitcast.5, bf16[256,256]{1,0:T(8,128)(2,1)} %emb_h.1, bf16[16,128]{1,0:T(8,128)(2,1)} %bitcast.6, bf16[4,2048]{1,0:T(4,128)(2,1)} %ce_h.1, f32[4]{0:T(128)} %agg_h.1, s32[256]{0:T(256)} %map_h.1, s32[1,256]{1,0:T(1,128)} %bitcast.7, ...), custom_call_target="tpu_custom_call" | custom-call | tf_op jit(solution)/shard_map/pallas_call | solution.py:517
  83.5 1.2 %reshape.15 = bf16[256,4,256]{2,1,0:T(4,128)(2,1)} reshape(bf16[256,1024]{1,0:T(8,128)(2,1)S(1)} %shard_map.118) | data formatting | bytes 1048576 | tf_op jit(solution)/shard_map/reshape | solution.py:600

commit v5 on v4

--- a/solution.py
+++ b/solution.py
@@ -66,6 +66,7 @@
     keep,
     px,
     wd,
+    dec,
     wg,
     b,
     pre,
@@ -266,8 +267,6 @@
     rdma(mine, mine, esem.at[0], rsem.at[2], at(ci, nxt)).start()
     rdma(mine, mine, esem.at[0], rsem.at[4], at(ci, prv)).start()
     rdma(mine, mine, esem.at[0], rsem.at[1], at(ypartner, cross_loc)).start()
-    rdma(mine, mine, esem.at[0], rsem.at[3], at(ypartner, diagonals[0])).start()
-    rdma(mine, mine, esem.at[0], rsem.at[5], at(ypartner, diagonals[1])).start()
 
     @pl.loop(1, 8)
     def _(step):
@@ -278,18 +277,23 @@
             to_partner(2)
             arrived(4)
             to_partner(4)
+            rdma(mine, mine, esem.at[0], rsem.at[3], at(ypartner, diagonals[0])).start()
+            rdma(mine, mine, esem.at[0], rsem.at[5], at(ypartner, diagonals[1])).start()
 
         @pl.when(step == 3)
         def _():
+            arrived(6)
+            to_partner(6)
             arrived(1)
             to_partner(1)
+
+        @pl.when(step == 4)
+        def _():
             arrived(3)
             pass_on(3, 7, nxt)
             to_partner(3)
-            arrived(6)
-            to_partner(6)
-
-        @pl.when(step == 4)
+
+        @pl.when(step == 5)
         def _():
             arrived(5)
             to_partner(5)
@@ -388,6 +392,9 @@
     def zdev(to):
         return at(ylo * 2 * ZS + to * 2 + core)
 
+    def ahead(n):
+        return (z + way * n + ZS) % ZS
+
     @pl.loop(0, 4)
     def _(t):
         mine = pl.ds(pl.multiple_of(ylo * 128, 128), 128)
@@ -397,18 +404,18 @@
         zf[t] = total
         zs[t] = total.astype(BF)
         for d in (8, 7, 6, 5):
-            to, via = (z + d) % ZS, (z + d - 4) % ZS
+            to, via = ahead(d), ahead(d - 4)
             rdma(zs.at[t, to], rin.at[t, 0, d - 5], zsem.at[0], rinsem.at[0, t], zdev(via)).start()
             if d < 8:
-                to, via = (z + ZS - d) % ZS, (z + ZS - d + 4) % ZS
+                to, via = ahead(-d), ahead(4 - d)
                 rdma(zs.at[t, to], rin.at[t, 1, d - 5], zsem.at[0], rinsem.at[1, t], zdev(via)).start()
         for d in (3, 2, 1):
-            for q, to in enumerate(((z + d) % ZS, (z + ZS - d) % ZS)):
+            for q, to in enumerate((ahead(d), ahead(-d))):
                 rdma(zs.at[t, to], zr.at[t, q, d - 1], zsem.at[0], zrsem.at[t], zdev(to)).start()
 
     @pl.loop(0, 4)
     def _(t):
-        for q, to, n in ((0, (z + 4) % ZS, 4), (1, (z + ZS - 4) % ZS, 3)):
+        for q, to, n in ((0, ahead(4), 4), (1, ahead(-4), 3)):
             await_bytes(rin.at[t, q, pl.ds(0, n)], rinsem.at[q, t])
             total = zf[t, to]
             for d in range(n):
@@ -434,13 +441,13 @@
     jt[core, ylo, z] = (scaled * inverse).astype(BF)
 
     def row_block(row, d):
-        return jt.at[core, row, (z + ZS - d) % ZS]
+        return jt.at[core, row, ahead(-d)]
 
     def spread(d, way_z, steps):
         for n in steps:
             block = row_block(ylo, d)
             there = (d + way_z * n) % ZS
-            rdma(block, block, jsem.at[0], jz.at[there], zdev((z + ZS + way_z * n) % ZS)).start()
+            rdma(block, block, jsem.at[0], jz.at[there], zdev(ahead(way_z * n))).start()
 
     def share_block(d):
         block = row_block(ylo, d)
@@ -459,30 +466,36 @@
         if d == 12:
             spread(12, -1, (3, 2, 1))
         share_block(d)
-    def decode(row):
-        sides = [jt[c, row].reshape(128, 1024) for c in range(2)]
+    def decode_own(row):
+        side = jt[core, row].reshape(128, 1024)
 
         @pl.loop(0, BUNDLE)
         def _(c):
-            total = jnp.dot(sides[0], wd[c, 0:1024, :], preferred_element_type=F32)
-            total = total + jnp.dot(sides[1], wd[c, 1024:2048, :], preferred_element_type=F32)
+            part = wd[c, pl.ds(pl.multiple_of(core * 1024, 1024), 1024), :]
+            dec[c] = jnp.dot(side, part, preferred_element_type=F32) + hbias[pl.ds(c, 1), :]
+
+    def decode_rest(row):
+        side = jt[1 - core, row].reshape(128, 1024)
+
+        @pl.loop(0, BUNDLE)
+        def _(c):
+            part = wd[c, pl.ds(pl.multiple_of((1 - core) * 1024, 1024), 1024), :]
             rows = pl.ds(pl.multiple_of(row * 128, 128), 128)
             columns = pl.ds(pl.multiple_of(c * BLOCK, BLOCK), BLOCK)
-            out[rows, columns] = (total + hbias[pl.ds(c, 1), :]).astype(BF)
-
+            out[rows, columns] = (dec[c] + jnp.dot(side, part, preferred_element_type=F32)).astype(BF)
+
+    decode_own(ylo)
     for d in range(ZS):
-        block = jt.at[1 - core, ylo, (z + ZS - d) % ZS]
-        await_bytes(block, jc.at[d])
-    decode(ylo)
+        await_bytes(jt.at[1 - core, ylo, ahead(d)], jc.at[d])
+    decode_rest(ylo)
     for d in (0, *order):
         block = row_block(1 - ylo, d)
         await_bytes(block, jy.at[d])
         rdma(block, block, jsem.at[2], jd.at[d], at(partner)).start()
-
+    decode_own(1 - ylo)
     for d in range(ZS):
-        block = jt.at[1 - core, 1 - ylo, (z + ZS - d) % ZS]
-        await_bytes(block, jd.at[d])
-    decode(1 - ylo)
+        await_bytes(jt.at[1 - core, 1 - ylo, ahead(d)], jd.at[d])
+    decode_rest(1 - ylo)
 
     await_bytes(wg.at[pl.ds(0, 7)], esem.at[0])
     await_bytes(sbuf.at[pl.ds(0, CHAN - 1)], ssem.at[0])
@@ -536,6 +549,7 @@
             pltpu.VMEM((BUNDLE, LOCS, 128), F32),
             pltpu.VMEM((BUNDLE * LOCS, BLOCK + 128), BF),
             pltpu.VMEM((BUNDLE, E, BLOCK), BF),
+            pltpu.VMEM((BUNDLE, 128, BLOCK), F32),
             pltpu.VMEM((8, 2, 128, BLOCK), BF),
             pltpu.VMEM((8, 2 * LOCS, BLOCK), BF),
             pltpu.VMEM((BUNDLE * LOCS, BLOCK), F32),

time: 84.8 us -> 83.4 us (0.983)
  Pallas kernels: 83.5 us -> 82.1 us
    pallas_call x1, Pallas kernels: 83.5 us -> 82.1 us  [shards(): pl.pallas_call(kernel, out_shape=jax.ShapeDtypeStruct((LOCS, BUNDLE * BLO...]
where the time goes in v5:
time: 83.4 us; the launch traced here: 83.3 us
  Pallas kernels  82.1 us (98%)
  local copies, waits for them, and re-layouts  1.17 us (1%)
    pallas_call x1, Pallas kernels, shards(): pl.pallas_call(kernel, out_shape=jax.ShapeDtypeStruct((LOCS, BUNDLE * BLO...  82.1 us

profile of v5, /device:TPU:1, one launch (start us, length us, event | category | flops | bytes accessed | tf_op | source)
XLA Modules:
  0.0 83.3 jit_solution(9085081924467012095)
XLA Ops:
  0.0 82.1 %shard_map.118 = bf16[256,1024]{1,0:T(8,128)(2,1)S(1)} custom-call(bf16[256,4,256]{2,1,0:T(4,128)(2,1)} %pixels_h.1, s32[4,256]{1,0:T(4,128)} %bitcast.5, bf16[256,256]{1,0:T(8,128)(2,1)} %emb_h.1, bf16[16,128]{1,0:T(8,128)(2,1)} %bitcast.6, bf16[4,2048]{1,0:T(4,128)(2,1)} %ce_h.1, f32[4]{0:T(128)} %agg_h.1, s32[256]{0:T(256)} %map_h.1, s32[1,256]{1,0:T(1,128)} %bitcast.7, ...), custom_call_target="tpu_custom_call" | custom-call | tf_op jit(solution)/shard_map/pallas_call | solution.py:530
  82.1 1.2 %reshape.15 = bf16[256,4,256]{2,1,0:T(4,128)(2,1)} reshape(bf16[256,1024]{1,0:T(8,128)(2,1)S(1)} %shard_map.118) | data formatting | bytes 1048576 | tf_op jit(solution)/shard_map/reshape | solution.py:614

commit v6 on v5

--- a/solution.py
+++ b/solution.py
@@ -246,7 +246,7 @@
         weight = jnp.concatenate([wg[j].reshape(BLOCK, BLOCK), extra.astype(BF)], axis=0)
         pre[...] = jnp.dot(px[...], weight, preferred_element_type=F32)
 
-        @pl.loop(0, LOCS // 32)
+        @pl.loop(0, LOCS // 32, unroll=True)
         def _(chunk):
             first, second = None, None
             for k in range(BUNDLE):
@@ -267,6 +267,7 @@
     rdma(mine, mine, esem.at[0], rsem.at[2], at(ci, nxt)).start()
     rdma(mine, mine, esem.at[0], rsem.at[4], at(ci, prv)).start()
     rdma(mine, mine, esem.at[0], rsem.at[1], at(ypartner, cross_loc)).start()
+    rdma(mine, mine, esem.at[0], rsem.at[3], at(ypartner, diagonals[0])).start()
 
     @pl.loop(1, 8)
     def _(step):
@@ -277,23 +278,22 @@
             to_partner(2)
             arrived(4)
             to_partner(4)
-            rdma(mine, mine, esem.at[0], rsem.at[3], at(ypartner, diagonals[0])).start()
             rdma(mine, mine, esem.at[0], rsem.at[5], at(ypartner, diagonals[1])).start()
 
-        @pl.when(step == 3)
+        @pl.when(step == 2)
         def _():
-            arrived(6)
-            to_partner(6)
             arrived(1)
             to_partner(1)
 
-        @pl.when(step == 4)
+        @pl.when(step == 3)
         def _():
             arrived(3)
             pass_on(3, 7, nxt)
             to_partner(3)
-
-        @pl.when(step == 5)
+            arrived(6)
+            to_partner(6)
+
+        @pl.when(step == 4)
         def _():
             arrived(5)
             to_partner(5)
@@ -303,7 +303,10 @@
             arrived(7)
             to_partner(7)
 
-        t, row = step % 4, step // 4
+        third = ((step // 3) % 2) * (1 - (step % 3 + 1) // 2)
+        fourth = (step // 4) * (1 - (step % 4 + 3) // 4)
+        turn = step + third - fourth
+        t, row = turn % 4, turn // 4
         j = place(t, row)
         await_bytes(wg.at[j, 1 - core], psem.at[2 * t + row])
         embed_block(j)
@@ -469,7 +472,7 @@
     def decode_own(row):
         side = jt[core, row].reshape(128, 1024)
 
-        @pl.loop(0, BUNDLE)
+        @pl.loop(0, BUNDLE, unroll=True)
         def _(c):
             part = wd[c, pl.ds(pl.multiple_of(core * 1024, 1024), 1024), :]
             dec[c] = jnp.dot(side, part, preferred_element_type=F32) + hbias[pl.ds(c, 1), :]
@@ -477,7 +480,7 @@
     def decode_rest(row):
         side = jt[1 - core, row].reshape(128, 1024)
 
-        @pl.loop(0, BUNDLE)
+        @pl.loop(0, BUNDLE, unroll=True)
         def _(c):
             part = wd[c, pl.ds(pl.multiple_of((1 - core) * 1024, 1024), 1024), :]
             rows = pl.ds(pl.multiple_of(row * 128, 128), 128)

time: 83.4 us -> 80 us (0.959)
  Pallas kernels: 82.1 us -> 78.7 us
    pallas_call x1, Pallas kernels: 82.1 us -> 78.7 us  [shards(): pl.pallas_call(kernel, out_shape=jax.ShapeDtypeStruct((LOCS, BUNDLE * BLO...]
where the time goes in v6:
time: 80 us; the launch traced here: 79.9 us
  Pallas kernels  78.7 us (98%)
  local copies, waits for them, and re-layouts  1.17 us (1%)
    pallas_call x1, Pallas kernels, shards(): pl.pallas_call(kernel, out_shape=jax.ShapeDtypeStruct((LOCS, BUNDLE * BLO...  78.7 us

profile of v6, /device:TPU:1, one launch (start us, length us, event | category | flops | bytes accessed | tf_op | source)
XLA Modules:
  0.0 79.9 jit_solution(1520619925947697174)
XLA Ops:
  0.0 78.7 %shard_map.118 = bf16[256,1024]{1,0:T(8,128)(2,1)S(1)} custom-call(bf16[256,4,256]{2,1,0:T(4,128)(2,1)} %pixels_h.1, s32[4,256]{1,0:T(4,128)} %bitcast.5, bf16[256,256]{1,0:T(8,128)(2,1)} %emb_h.1, bf16[16,128]{1,0:T(8,128)(2,1)} %bitcast.6, bf16[4,2048]{1,0:T(4,128)(2,1)} %ce_h.1, f32[4]{0:T(128)} %agg_h.1, s32[256]{0:T(256)} %map_h.1, s32[1,256]{1,0:T(1,128)} %bitcast.7, ...), custom_call_target="tpu_custom_call" | custom-call | tf_op jit(solution)/shard_map/pallas_call | solution.py:533
  78.7 1.2 %reshape.15 = bf16[256,4,256]{2,1,0:T(4,128)(2,1)} reshape(bf16[256,1024]{1,0:T(8,128)(2,1)S(1)} %shard_map.118) | data formatting | bytes 1048576 | tf_op jit(solution)/shard_map/reshape | solution.py:617

commit v7 on v6

--- a/solution.py
+++ b/solution.py
@@ -378,12 +378,12 @@
         spread = jnp.dot(lhs[...], expand[j], preferred_element_type=F32)
         return spread[:LOCS] * b[j, 0:LOCS, :].astype(F32) + spread[LOCS:] * b[j, LOCS:, :].astype(F32)
 
-    @pl.loop(0, 4)
+    @pl.loop(0, 4, unroll=True)
     def _(t):
         ps[t] = weigh((1 - core) * 4 + t).astype(BF)
         rdma(ps.at[t], pr.at[t], csem.at[0], crsem.at[t], at(partner)).start()
 
-    @pl.loop(0, 4)
+    @pl.loop(0, 4, unroll=True)
     def _(t):
         mixed_in = weigh(core * 4 + t)
         await_bytes(pr.at[t], crsem.at[t])
@@ -398,7 +398,7 @@
     def ahead(n):
         return (z + way * n + ZS) % ZS
 
-    @pl.loop(0, 4)
+    @pl.loop(0, 4, unroll=True)
     def _(t):
         mine = pl.ds(pl.multiple_of(ylo * 128, 128), 128)
         await_bytes(yr.at[t], yrsem.at[t])
@@ -416,7 +416,7 @@
             for q, to in enumerate((ahead(d), ahead(-d))):
                 rdma(zs.at[t, to], zr.at[t, q, d - 1], zsem.at[0], zrsem.at[t], zdev(to)).start()
 
-    @pl.loop(0, 4)
+    @pl.loop(0, 4, unroll=True)
     def _(t):
         for q, to, n in ((0, ahead(4), 4), (1, ahead(-4), 3)):
             await_bytes(rin.at[t, q, pl.ds(0, n)], rinsem.at[q, t])

time: 80 us -> 80.2 us (level)
  no operation moved by 1% of the time
where the time goes in v7:
time: 80.2 us; the launch traced here: 80 us
  Pallas kernels  78.9 us (98%)
  local copies, waits for them, and re-layouts  1.17 us (1%)
    pallas_call x1, Pallas kernels, shards(): pl.pallas_call(kernel, out_shape=jax.ShapeDtypeStruct((LOCS, BUNDLE * BLO...  78.9 us

profile of v7, /device:TPU:1, one launch (start us, length us, event | category | flops | bytes accessed | tf_op | source)
XLA Modules:
  0.0 80.0 jit_solution(2335899964935808238)
XLA Ops:
  0.0 78.9 %shard_map.118 = bf16[256,1024]{1,0:T(8,128)(2,1)S(1)} custom-call(bf16[256,4,256]{2,1,0:T(4,128)(2,1)} %pixels_h.1, s32[4,256]{1,0:T(4,128)} %bitcast.5, bf16[256,256]{1,0:T(8,128)(2,1)} %emb_h.1, bf16[16,128]{1,0:T(8,128)(2,1)} %bitcast.6, bf16[4,2048]{1,0:T(4,128)(2,1)} %ce_h.1, f32[4]{0:T(128)} %agg_h.1, s32[256]{0:T(256)} %map_h.1, s32[1,256]{1,0:T(1,128)} %bitcast.7, ...), custom_call_target="tpu_custom_call" | custom-call | tf_op jit(solution)/shard_map/pallas_call | solution.py:533
  78.9 1.2 %reshape.15 = bf16[256,4,256]{2,1,0:T(4,128)(2,1)} reshape(bf16[256,1024]{1,0:T(8,128)(2,1)S(1)} %shard_map.118) | data formatting | bytes 1048576 | tf_op jit(solution)/shard_map/reshape | solution.py:617

commit v8 on v6

--- a/solution.py
+++ b/solution.py
@@ -461,7 +461,7 @@
         spread(0, 1, (n,))
         spread(0, -1, (n,))
     share_block(0)
-    order = (4, 12, 1, 15, 2, 14, 3, 13, 5, 11, 6, 10, 7, 9, 8)
+    order = (1, 15, 4, 12, 2, 14, 3, 13, 5, 11, 6, 10, 7, 9, 8)
     for d in order:
         await_bytes(row_block(ylo, d), jz.at[d])
         if d == 4:

time: 80 us -> 80.7 us (level)
  no operation moved by 1% of the time
where the time goes in v8:
time: 80.7 us; the launch traced here: 80.6 us
  Pallas kernels  79.4 us (98%)
  local copies, waits for them, and re-layouts  1.17 us (1%)
    pallas_call x1, Pallas kernels, shards(): pl.pallas_call(kernel, out_shape=jax.ShapeDtypeStruct((LOCS, BUNDLE * BLO...  79.4 us

profile of v8, /device:TPU:1, one launch (start us, length us, event | category | flops | bytes accessed | tf_op | source)
XLA Modules:
  0.0 80.6 jit_solution(1506860301894620207)
XLA Ops:
  0.0 79.4 %shard_map.118 = bf16[256,1024]{1,0:T(8,128)(2,1)S(1)} custom-call(bf16[256,4,256]{2,1,0:T(4,128)(2,1)} %pixels_h.1, s32[4,256]{1,0:T(4,128)} %bitcast.5, bf16[256,256]{1,0:T(8,128)(2,1)} %emb_h.1, bf16[16,128]{1,0:T(8,128)(2,1)} %bitcast.6, bf16[4,2048]{1,0:T(4,128)(2,1)} %ce_h.1, f32[4]{0:T(128)} %agg_h.1, s32[256]{0:T(256)} %map_h.1, s32[1,256]{1,0:T(1,128)} %bitcast.7, ...), custom_call_target="tpu_custom_call" | custom-call | tf_op jit(solution)/shard_map/pallas_call | solution.py:533
  79.4 1.2 %reshape.15 = bf16[256,4,256]{2,1,0:T(4,128)(2,1)} reshape(bf16[256,1024]{1,0:T(8,128)(2,1)S(1)} %shard_map.118) | data formatting | bytes 1048576 | tf_op jit(solution)/shard_map/reshape | solution.py:617
